TPU v7x, 32 devices: a whole 2x2x4 slice. The times are simulated.
32 devices in a mesh: gx: 4 (over y, core), gy: 8 (over z, x).
Axes of the slice: x: 2, y: 2, z: 4, core: 2. Of those that a mesh axis runs over, the one named last changes fastest.
Arguments:
- features: bfloat16 [4, 8, 128, 256], P('gx', 'gy'), may hold values from -6 to 6
- occupancy: int32 [4, 8, 128], P('gx', 'gy'), may hold values from 0 to 1, as said below
- coords: int32 [4, 8, 3, 128], P('gx', 'gy'), may hold values from 0 to 7, as said below
- norm_gains: float32 [2, 2, 256], replicated, may hold values from 0.1 to 1.9
- bias_tables: float32 [2, 3, 8, 15], replicated, may hold values from -4 to 4
- w_qkv: bfloat16 [2, 256, 768], replicated, may hold values from -0.375 to 0.375
- w_out: bfloat16 [2, 256, 256], replicated, may hold values from -0.375 to 0.375
- w_up: bfloat16 [2, 256, 1024], replicated, may hold values from -0.375 to 0.375
- w_down: bfloat16 [2, 1024, 256], replicated, may hold values from -0.1875 to 0.1875
- grad_out: bfloat16 [4, 8, 128, 256], P('gx', 'gy'), may hold values from -6 to 6
Outputs:
- out_points: bfloat16 [4, 8, 128, 256], P('gx', 'gy')
- grad_points: bfloat16 [4, 8, 128, 256], P('gx', 'gy')
- grad_tables: float32 [2, 3, 8, 15], replicated
Inputs may be any that keep to these rules, and one draw needn't show every extreme that they name: `occupancy`: 1 marks an occupied slot. In each quarter of 32 slots of a window the occupied slots come first, and every quarter holds at least one. `coords`: the x coordinate of a slot of quarter (a, b) lies in [a * 4, (a + 1) * 4) and its y coordinate in [b * 4, (b + 1) * 4); z lies in [0, 8).
All inputs are finite; a program needn't handle non-finite values.
Results may differ from a plain program's by a relative error of at most 0.02.
Values may be sent and summed in bfloat16 or wider, within the bound.
A program may use at most 64 MiB of HBM per device.

v0:
```python
from functools import partial

import jax
import jax.numpy as jnp
from jax import lax
from jax.sharding import PartitionSpec as P

highest_precision = lax.Precision.HIGHEST
epsilon = 1e-05


def from_behind(value, axis, steps):
    count = lax.axis_size(axis)
    pairs = [(source, (source + steps) % count) for source in range(count)]
    return lax.ppermute(value, axis, pairs)


def layer_norm(values, gain):
    mean_value = jnp.mean(values, axis=-1, keepdims=True)
    centred = values - mean_value
    variance = jnp.mean(centred * centred, axis=-1, keepdims=True)
    return centred * lax.rsqrt(variance + epsilon) * gain


def relative_bias(coords, bias_table):
    table_span = bias_table.shape[-1]
    window_span = (table_span + 1) // 2
    cell_index = jnp.arange(window_span, dtype=jnp.int32)
    offsets = cell_index[:, None] - cell_index[None, :] + window_span - 1
    selection_matrix = (
        offsets[:, :, None] == jnp.arange(table_span, dtype=jnp.int32)[None, None, :]
    ).astype(jnp.float32)
    total = None
    for axis_index in range(3):
        indicator_matrix = (coords[axis_index][:, None] == cell_index[None, :]).astype(jnp.float32)
        banded_offset_matrix = jnp.einsum(
            "hr,abr->hab", bias_table[axis_index], selection_matrix, precision=highest_precision
        )
        left_factor = jnp.einsum(
            "dx,cxq->cdq", indicator_matrix, banded_offset_matrix, precision=highest_precision
        )
        axis_contribution_part = jnp.einsum(
            "klu,tu->klt", left_factor, indicator_matrix, precision=highest_precision
        )
        total = axis_contribution_part if total is None else total + axis_contribution_part
    return total


def attend(queries, keys_part, values_part, bias_table, occupied, coords):
    head_size = queries.shape[-1]
    scores = jnp.einsum("qhd,khd->hqk", queries, keys_part, preferred_element_type=jnp.float32)
    scores = scores * head_size ** (-0.5) + relative_bias(coords, bias_table)
    scores = jnp.where(occupied[None, None, :] > 0, scores, -1e30)
    weights_soft = jax.nn.softmax(scores, axis=-1).astype(jnp.bfloat16)
    mixed = jnp.einsum(
        "hqk,khd->qhd", weights_soft, values_part, preferred_element_type=jnp.float32
    )
    return mixed.reshape(mixed.shape[0], -1).astype(jnp.bfloat16)


def swin_block(
    hidden,
    bias_table,
    occupied,
    coords,
    gains,
    weight_qkv,
    weight_out,
    up_weight_matrix,
    weight_down,
):
    slots, width = hidden.shape
    heads = bias_table.shape[1]
    core = jax.checkpoint(partial(attend, occupied=occupied, coords=coords))
    normed = layer_norm(hidden.astype(jnp.float32), gains[0]).astype(jnp.bfloat16)
    projected = jnp.dot(normed, weight_qkv, preferred_element_type=jnp.float32).astype(jnp.bfloat16)
    qkv_parts = projected.reshape(slots, 3, heads, width // heads)
    mixed = core(qkv_parts[:, 0], qkv_parts[:, 1], qkv_parts[:, 2], bias_table)
    middle = hidden.astype(jnp.float32) + jnp.dot(
        mixed, weight_out, preferred_element_type=jnp.float32
    )
    normed_two = layer_norm(middle, gains[1]).astype(jnp.bfloat16)
    expanded = jax.nn.gelu(
        jnp.dot(normed_two, up_weight_matrix, preferred_element_type=jnp.float32)
    ).astype(jnp.bfloat16)
    return (middle + jnp.dot(expanded, weight_down, preferred_element_type=jnp.float32)).astype(
        jnp.bfloat16
    )


def run_block(
    occupied,
    coords,
    gains,
    weight_qkv,
    weight_out,
    up_weight_matrix,
    weight_down,
    hidden,
    bias_table,
):
    return swin_block(
        hidden,
        bias_table,
        occupied,
        coords,
        gains,
        weight_qkv,
        weight_out,
        up_weight_matrix,
        weight_down,
    )


def roll_half(array, position, step_sign, sender):
    lower_half = lax.index_in_dim(array, 0, position, keepdims=False)
    upper_half = lax.index_in_dim(array, 1, position, keepdims=False)
    if step_sign < 0:
        return jnp.stack([upper_half, sender(lower_half, step_sign)], axis=position)
    return jnp.stack([sender(upper_half, step_sign), lower_half], axis=position)


def send_values_y_first(piece, step_sign):
    return from_behind(piece, "gy", step_sign)


def send_values_x_second(piece, step_sign):
    return from_behind(piece, "gx", step_sign)


def send_meta_x(piece, step_sign):
    return from_behind(piece, "gx", step_sign)


def send_meta_y(piece, step_sign):
    return from_behind(piece, "gy", step_sign)


def roll_values(points, step_sign):
    slots, width = points.shape
    tiles = points.reshape(2, 2, slots // 4, width)
    tiles = roll_half(tiles, 1, step_sign, send_values_y_first)
    tiles = roll_half(tiles, 0, step_sign, send_values_x_second)
    return tiles.reshape(slots, width)


def on_device(
    features, occupancy, coords, norm_gains, bias_tables, w_qkv, w_out, w_up, w_down, grad_out
):
    points = features[0, 0]
    slots, width = points.shape
    quarter = slots // 4
    window_span = (bias_tables.shape[-1] + 1) // 2
    half_span = window_span // 2
    local_coords = coords[0, 0]
    slot_meta = jnp.concatenate([occupancy[0, 0][None], local_coords], axis=0).reshape(
        4, 2, 2, quarter
    )
    slot_meta = roll_half(slot_meta, 1, -1, send_meta_x)
    slot_meta = roll_half(slot_meta, 2, -1, send_meta_y)
    slot_meta = slot_meta.reshape(4, slots)
    shifted_coords = jnp.stack(
        [
            (slot_meta[1] + half_span) % window_span,
            (slot_meta[2] + half_span) % window_span,
            slot_meta[3],
        ],
        axis=0,
    )
    occupied = occupancy[0, 0].astype(jnp.float32)
    shifted_occupied = slot_meta[0].astype(jnp.float32)
    occupied_mask = occupancy[0, 0].astype(jnp.bfloat16)[:, None]
    first_out, pullback_first_block = jax.vjp(
        partial(
            run_block, occupied, local_coords, norm_gains[0], w_qkv[0], w_out[0], w_up[0], w_down[0]
        ),
        points,
        bias_tables[0],
    )
    rolled = roll_values(first_out, -1)
    second, pull_second = jax.vjp(
        partial(
            run_block,
            shifted_occupied,
            shifted_coords,
            norm_gains[1],
            w_qkv[1],
            w_out[1],
            w_up[1],
            w_down[1],
        ),
        rolled,
        bias_tables[1],
    )
    out_points = roll_values(second, 1) * occupied_mask
    grad_masked = grad_out[0, 0] * occupied_mask
    grad_second = roll_values(grad_masked, -1)
    grad_rolled, table_second = pull_second(grad_second)
    grad_first = roll_values(grad_rolled, 1)
    grad_points, table_first = pullback_first_block(grad_first)
    grad_tables = lax.psum(jnp.stack([table_first, table_second]), ("gx", "gy"))
    return (out_points[None, None], grad_points[None, None], grad_tables)


def solution(mesh):
    return jax.shard_map(
        on_device,
        mesh=mesh,
        in_specs=(
            P("gx", "gy", None, None),
            P("gx", "gy", None),
            P("gx", "gy", None, None),
            P(),
            P(),
            P(),
            P(),
            P(),
            P(),
            P("gx", "gy", None, None),
        ),
        out_specs=(P("gx", "gy", None, None), P("gx", "gy", None, None), P()),
        check_vma=False,
    )
```

profile of v0, /device:TPU:0, one launch (start us, length us, event | category | flops | bytes accessed | tf_op | source)
XLA Modules:
  0.0 126.7 jit_solution(14831470220419939632)
XLA Ops:
  1.2 2.0 %convert_bitcast_fusion.2 = (f32[128]{0:T(128)}, bf16[128]{0:T(256)(128)(2,1)}, s32[128]{0:T(128)S(1)}) fusion(s32[1,1,128]{2,1,0:T(1,128)} %param.11, s32[]{:T(128)} %broadcast.665), kind=kLoop, calls=%fused_computation.514 | loop fusion | flops 256 | bytes 1796 | tf_op jit(solution)/shard_map/convert_element_type | solution.py:170
  3.2 0.7 reduce.4
  4.0 2.5 %collective-permute-start.2 = (s32[4,2,32]{2,0,1:T(4,128)S(1)}, s32[4,2,32]{2,0,1:T(4,128)S(1)}, u32[]{:S(2)}, u32[]{:S(2)}) collective-permute-start(s32[4,2,32]{2,0,1:T(4,128)S(1)} %get-tuple-element.56), channel_id=1, source_target_pairs={{0,24},{8,0},{16,8},{24,16},{1,25},{9,1},{17,9},{25,17},{2,26},{10... | collective-permute-start | bytes 3080 | tf_op jit(solution)/shard_map/ppermute | solution.py:15
  6.5 0.7 convert_reduce_fusion.2
  7.4 4.6 %collective-permute-start.6 = (bf16[2,32,256]{2,1,0:T(8,128)(2,1)S(1)}, bf16[2,32,256]{2,1,0:T(8,128)(2,1)S(1)}, u32[]{:S(2)}, u32[]{:S(2)}) collective-permute-start(bf16[2,32,256]{2,1,0:T(8,128)(2,1)S(1)} %get-tuple-element.46), channel_id=1, source_target_pairs={{0,7},{1,0},{2,1},{3,2},{4,3},{5,4},{6,5},{7,6},{8,15},{9,8},{10,9... | collective-permute-start | bytes 98312 | tf_op jit(solution)/shard_map/ppermute | solution.py:15
  14.6 1.2 convolution_convert_fusion.5
  18.5 0.7 copy-done.2
  22.8 0.6 slice_bitcast_fusion.5
  23.7 1.4 %collective-permute-start.3 = (s32[4,2,32]{2,1,0:T(2,128)S(1)}, s32[4,2,32]{2,1,0:T(2,128)S(1)}, u32[]{:S(2)}, u32[]{:S(2)}) collective-permute-start(s32[4,2,32]{2,1,0:T(2,128)S(1)} %get-tuple-element.62), channel_id=1, source_target_pairs={{0,7},{1,0},{2,1},{3,2},{4,3},{5,4},{6,5},{7,6},{8,15},{9,8},{10,9... | collective-permute-start | bytes 3080 | tf_op jit(solution)/shard_map/ppermute | solution.py:15
  25.1 0.6 slice_bitcast_fusion.12
  26.5 0.8 collective-permute-done.3
  29.5 0.7 collective-permute-start.7
  30.2 0.8 collective-permute-done.1
  34.2 0.9 fusion.25
  35.2 0.6 div.153
  35.8 1.8 %multiply_reduce_fusion.4 = (f32[128]{0:T(128)S(1)}, f32[128,256]{1,0:T(8,128)S(1)}) fusion(f32[128,256]{1,0:T(8,128)S(1)} %get-tuple-element.86, f32[128]{0:T(128)S(1)} %broadcast_multiply_fusion.2, f32[256]{0:T(256)S(1)} %bitcast.558, bf16[2,256,1024]{2,1,0:T(8,128)(2,1)S(1)} %copy-done.1, f32[128,1024]{1,0:T(8,128)S(1)} %fusion.57, ...), kind=kOutput, calls=%fused_computation.237 | convolution fusion | flops 137166720 | bytes 1902592 | tf_op jit(solution)/shard_map/transpose(jvp())/dot_general | solution.py:84
  42.7 0.9 fusion.34
  44.0 0.8 fusion.37
  44.8 0.9 fusion.36
  47.5 0.7 add.251
  48.2 1.4 %slice_bitcast_fusion.9 = (bf16[2,32,256]{2,1,0:T(8,128)(2,1)}, bf16[2,1,32,256]{3,2,1,0:T(8,128)(2,1)S(1)}) fusion(bf16[2,2,32,256]{3,2,1,0:T(8,128)(2,1)} %bitcast.540), kind=kLoop, calls=%fused_computation.300 | loop fusion | bytes 131072 | tf_op jit(solution)/shard_map/squeeze | solution.py:117
  49.6 2.3 %collective-permute-start.4 = (bf16[2,32,256]{2,1,0:T(8,128)(2,1)}, bf16[2,32,256]{2,1,0:T(8,128)(2,1)S(1)}, u32[]{:S(2)}, u32[]{:S(2)}) collective-permute-start(bf16[2,32,256]{2,1,0:T(8,128)(2,1)} %get-tuple-element.47), channel_id=1, source_target_pairs={{0,1},{1,2},{2,3},{3,4},{4,5},{5,6},{6,7},{7,0},{8,9},{9,10},{10,1... | collective-permute-start | bytes 98312 | tf_op jit(solution)/shard_map/ppermute | solution.py:15
  51.9 0.9 pad_add_fusion.1
  52.8 0.6 copy-done.24
  53.4 1.4 %multiply_reduce_fusion.3 = (f32[128]{0:T(128)S(1)}, f32[128,256]{1,0:T(8,128)S(1)}) fusion(f32[128]{0:T(128)S(1)} %copy-done.24, bf16[1,2,32,256]{3,2,1,0:T(8,128)(2,1)S(1)} %bitcast.518, bf16[1,2,32,256]{3,2,1,0:T(8,128)(2,1)S(1)} %get-tuple-element.49, f32[256]{0:T(256)S(1)} %bitcast.556, bf16[128,768]{0,1:T(8,128)(2,1)S(1)} %bitcast.533, ...), kind=kOutput, calls=%fused_computation.235 | convolution fusion | flops 50593664 | bytes 788480 | tf_op jit(solution)/shard_map/transpose(jvp())/dot_general | solution.py:76
  54.8 0.7 copy-done.35
  58.0 0.6 fusion.280
  58.9 0.6 fusion.286
  59.8 3.4 %collective-permute-done.8 = bf16[2,32,256]{2,1,0:T(8,128)(2,1)S(1)} collective-permute-done((bf16[2,32,256]{2,1,0:T(8,128)(2,1)S(1)}, bf16[2,32,256]{2,1,0:T(8,128)(2,1)S(1)}, u32[]{:S(2)}, u32[]{:S(2)}) %collective-permute-start.8) | collective-permute-done | bytes 32800 | tf_op jit(solution)/shard_map/ppermute | solution.py:15
  63.2 0.8 collective-permute-start.5
  64.0 2.5 %collective-permute-done.9 = bf16[2,32,256]{2,1,0:T(8,128)(2,1)S(1)} collective-permute-done((bf16[2,32,256]{2,1,0:T(8,128)(2,1)S(1)}, bf16[2,32,256]{2,1,0:T(8,128)(2,1)S(1)}, u32[]{:S(2)}, u32[]{:S(2)}) %collective-permute-start.9) | collective-permute-done | bytes 32800 | tf_op jit(solution)/shard_map/ppermute | solution.py:15
  66.5 0.6 copy-done.21
  67.2 1.8 %multiply_reduce_fusion.2 = (f32[128]{0:T(128)S(1)}, f32[128,256]{1,0:T(8,128)S(1)}) fusion(f32[128,256]{1,0:T(8,128)S(1)} %get-tuple-element.84, f32[128]{0:T(128)S(1)} %copy-done.21, f32[256]{0:T(256)S(1)} %bitcast.554, bf16[2,256,1024]{2,1,0:T(8,128)(2,1)S(1)} %copy-done.1, f32[128,1024]{1,0:T(8,128)S(1)} %copy-done.8, ...), kind=kOutput, calls=%fused_computation.233 | convolution fusion | flops 137166720 | bytes 1902592 | tf_op jit(solution)/shard_map/transpose(jvp())/dot_general | solution.py:84
  69.0 0.6 copy-done.45
  69.6 0.7 copy-done.33
  76.5 0.7 copy-done.4
  77.6 0.6 convolution_bitcast_fusion.3
  80.3 0.6 copy-done.23
  80.9 1.4 %fusion.147 = (f32[128]{0:T(128)S(1)}, f32[128,256]{1,0:T(8,128)S(1)}) fusion(bf16[1,1,128,256]{3,2,1,0:T(8,128)(2,1)S(1)} %copy-done, f32[128]{0:T(128)S(1)} %copy-done.23, f32[256]{0:T(256)S(1)} %bitcast.562, bf16[128,768]{0,1:T(8,128)(2,1)S(1)} %bitcast.534, bf16[2,256,768]{2,1,0:T(8,128)(2,1)} %param.15), kind=kOutput, calls=%fused_computation.222 | convolution fusion | flops 50560896 | bytes 788480 | tf_op jit(solution)/shard_map/transpose(jvp())/dot_general | solution.py:76
  82.3 0.7 copy-done.43
  83.0 0.6 copy-done.37
  83.8 0.6 copy-done.6
  84.5 0.8 fusion.162
  86.1 0.6 fusion.299
  87.0 0.6 fusion.305
  88.0 37.3 %psum.7 = f32[2,3,8,15]{3,2,1,0:T(8,128)} all-reduce(f32[2,3,8,15]{3,2,1,0:T(8,128)S(1)} %pad_maximum_fusion.6), channel_id=1, replica_groups=mesh['gx'=4,'gy'=8] {'gx','gy'}, use_global_device_ids=true, to_apply=%region_26.27 | all-reduce | flops 720 | bytes 5760 | tf_op jit(solution)/shard_map/psum | solution.py:201
  125.3 0.7 copy-done.34
  125.9 0.7 broadcast_multiply_fusion
  (267 shorter events, 36.1 us)
Async XLA Ops:
  0.6 6.7 %copy-start.15 = (bf16[1,1,128,256]{3,2,1,0:T(8,128)(2,1)S(1)}, bf16[1,1,128,256]{3,2,1,0:T(8,128)(2,1)}, u32[]{:S(2)}) copy-start(bf16[1,1,128,256]{3,2,1,0:T(8,128)(2,1)} %param.19) | copy-start | bytes 196612
  4.0 19.6 %collective-permute-start.2 = (s32[4,2,32]{2,0,1:T(4,128)S(1)}, s32[4,2,32]{2,0,1:T(4,128)S(1)}, u32[]{:S(2)}, u32[]{:S(2)}) collective-permute-start(s32[4,2,32]{2,0,1:T(4,128)S(1)} %get-tuple-element.56), channel_id=1, source_target_pairs={{0,24},{8,0},{16,8},{24,16},{1,25},{9,1},{17,9},{25,17},{2,26},{10... | collective-permute-start | bytes 3080 | tf_op jit(solution)/shard_map/ppermute | solution.py:15
  7.4 4.6 %copy-start.46 = (s32[1,1,128]{2,1,0:T(1,128)S(1)}, s32[1,1,128]{2,1,0:T(1,128)}, u32[]{:S(2)}) copy-start(s32[1,1,128]{2,1,0:T(1,128)} %param.11) | copy-start | bytes 1540
  7.4 4.7 %copy-start.16 = (f32[2,3,8,15]{3,2,1,0:T(8,128)S(1)}, f32[2,3,8,15]{3,2,1,0:T(8,128)}, u32[]{:S(2)}) copy-start(f32[2,3,8,15]{3,2,1,0:T(8,128)} %param.14) | copy-start | bytes 8644
  7.4 4.6 %copy-start.17 = (s32[1,1,3,128]{3,1,2,0:T(1,128)S(1)}, s32[1,1,3,128]{3,1,2,0:T(1,128)}, u32[]{:S(2)}) copy-start(s32[1,1,3,128]{3,1,2,0:T(1,128)} %param.12) | copy-start | bytes 4612
  7.4 22.0 %collective-permute-start.6 = (bf16[2,32,256]{2,1,0:T(8,128)(2,1)S(1)}, bf16[2,32,256]{2,1,0:T(8,128)(2,1)S(1)}, u32[]{:S(2)}, u32[]{:S(2)}) collective-permute-start(bf16[2,32,256]{2,1,0:T(8,128)(2,1)S(1)} %get-tuple-element.46), channel_id=1, source_target_pairs={{0,7},{1,0},{2,1},{3,2},{4,3},{5,4},{6,5},{7,6},{8,15},{9,8},{10,9... | collective-permute-start | bytes 98312 | tf_op jit(solution)/shard_map/ppermute | solution.py:15
  12.1 27.3 %copy-start.30 = (s32[8,8]{1,0:T(8,128)}, s32[8,8]{1,0:T(8,128)S(1)}, u32[]{:S(2)}) copy-start(s32[8,8]{1,0:T(8,128)S(1)} %subtract_add_fusion) | copy-start | bytes 772
  12.3 0.8 copy-start
  13.2 1.1 copy-start.22
  13.3 0.8 copy-start.29
  14.1 6.1 %copy-start.25 = (f32[1,1,256]{2,1,0:T(1,128)}, f32[1,1,256]{2,1,0:T(1,128)S(1)}, u32[]{:S(2)}) copy-start(f32[1,1,256]{2,1,0:T(1,128)S(1)} %get-tuple-element.64) | copy-start | bytes 3076
  14.1 17.3 %copy-start.27 = (f32[1,1,256]{2,1,0:T(1,128)}, f32[1,1,256]{2,1,0:T(1,128)S(1)}, u32[]{:S(2)}) copy-start(f32[1,1,256]{2,1,0:T(1,128)S(1)} %get-tuple-element.66) | copy-start | bytes 3076
  18.2 1.0 copy-start.2
  18.2 2.5 %copy-start.1 = (bf16[2,256,1024]{2,1,0:T(8,128)(2,1)S(1)}, bf16[2,256,1024]{2,1,0:T(8,128)(2,1)}, u32[]{:S(2)}) copy-start(bf16[2,256,1024]{2,1,0:T(8,128)(2,1)} %param.17) | copy-start | bytes 3145732
  18.4 2.6 %copy-start.48 = (bf16[2,1024,256]{2,1,0:T(8,128)(2,1)S(1)}, bf16[2,1024,256]{2,1,0:T(8,128)(2,1)}, u32[]{:S(2)}) copy-start(bf16[2,1024,256]{2,1,0:T(8,128)(2,1)} %param.18) | copy-start | bytes 3145732
  19.4 0.7 copy-start.20
  21.0 0.8 copy-start.7
  21.8 7.5 %collective-permute-start = (bf16[2,32,256]{2,1,0:T(8,128)(2,1)S(1)}, bf16[2,32,256]{2,1,0:T(8,128)(2,1)S(1)}, u32[]{:S(2)}, u32[]{:S(2)}) collective-permute-start(bf16[2,32,256]{2,1,0:T(8,128)(2,1)S(1)} %get-tuple-element.52), channel_id=1, source_target_pairs={{0,7},{1,0},{2,1},{3,2},{4,3},{5,4},{6,5},{7,6},{8,15},{9,8},{10,9... | collective-permute-start | bytes 98312 | tf_op jit(solution)/shard_map/ppermute | solution.py:15
  23.5 51.0 %copy-start.3 = (bf16[128,8,32]{0,2,1:T(8,128)(2,1)}, bf16[128,8,32]{0,2,1:T(8,128)(2,1)S(1)}, u32[]{:S(2)}) copy-start(bf16[128,8,32]{0,2,1:T(8,128)(2,1)S(1)} %get-tuple-element.27) | copy-start | bytes 196612
  23.7 3.7 %collective-permute-start.3 = (s32[4,2,32]{2,1,0:T(2,128)S(1)}, s32[4,2,32]{2,1,0:T(2,128)S(1)}, u32[]{:S(2)}, u32[]{:S(2)}) collective-permute-start(s32[4,2,32]{2,1,0:T(2,128)S(1)} %get-tuple-element.62), channel_id=1, source_target_pairs={{0,7},{1,0},{2,1},{3,2},{4,3},{5,4},{6,5},{7,6},{8,15},{9,8},{10,9... | collective-permute-start | bytes 3080 | tf_op jit(solution)/shard_map/ppermute | solution.py:15
  28.9 2.6 %copy-start.14 = (bf16[2,256,768]{2,1,0:T(8,128)(2,1)S(1)}, bf16[2,256,768]{2,1,0:T(8,128)(2,1)}, u32[]{:S(2)}) copy-start(bf16[2,256,768]{2,1,0:T(8,128)(2,1)} %param.15) | copy-start | bytes 2359300
  29.4 1.7 %collective-permute-start.1 = (bf16[2,32,256]{2,1,0:T(8,128)(2,1)S(1)}, bf16[2,32,256]{2,1,0:T(8,128)(2,1)S(1)}, u32[]{:S(2)}, u32[]{:S(2)}) collective-permute-start(bf16[2,32,256]{2,1,0:T(8,128)(2,1)S(1)} %get-tuple-element.50), channel_id=1, source_target_pairs={{0,24},{8,0},{16,8},{24,16},{1,25},{9,1},{17,9},{25,17},{2,26},{10... | collective-permute-start | bytes 98312 | tf_op jit(solution)/shard_map/ppermute | solution.py:15
  29.5 6.4 %collective-permute-start.7 = (bf16[2,32,256]{2,1,0:T(8,128)(2,1)S(1)}, bf16[2,32,256]{2,1,0:T(8,128)(2,1)S(1)}, u32[]{:S(2)}, u32[]{:S(2)}) collective-permute-start(bf16[2,32,256]{2,1,0:T(8,128)(2,1)S(1)} %get-tuple-element.44), channel_id=1, source_target_pairs={{0,24},{8,0},{16,8},{24,16},{1,25},{9,1},{17,9},{25,17},{2,26},{10... | collective-permute-start | bytes 98312 | tf_op jit(solution)/shard_map/ppermute | solution.py:15
  33.0 1.2 copy-start.49
  48.2 3.8 %copy-start.12 = (bf16[128,1,8,32]{0,3,2,1:T(8,128)(2,1)S(1)}, bf16[128,1,8,32]{0,3,2,1:T(8,128)(2,1)}, u32[]{:S(2)}) copy-start(bf16[128,1,8,32]{0,3,2,1:T(8,128)(2,1)} %fusion.37) | copy-start | bytes 196612
  48.2 3.8 %copy-start.13 = (bf16[128,1,8,32]{0,3,2,1:T(8,128)(2,1)S(1)}, bf16[128,1,8,32]{0,3,2,1:T(8,128)(2,1)}, u32[]{:S(2)}) copy-start(bf16[128,1,8,32]{0,3,2,1:T(8,128)(2,1)} %fusion.36) | copy-start | bytes 196612
  49.6 13.6 %copy-start.9 = (bf16[2,1,32,256]{3,2,1,0:T(8,128)(2,1)}, bf16[2,1,32,256]{3,2,1,0:T(8,128)(2,1)S(1)}, u32[]{:S(2)}) copy-start(bf16[2,1,32,256]{3,2,1,0:T(8,128)(2,1)S(1)} %get-tuple-element.48) | copy-start | bytes 98308
  49.6 13.6 %collective-permute-start.4 = (bf16[2,32,256]{2,1,0:T(8,128)(2,1)}, bf16[2,32,256]{2,1,0:T(8,128)(2,1)S(1)}, u32[]{:S(2)}, u32[]{:S(2)}) collective-permute-start(bf16[2,32,256]{2,1,0:T(8,128)(2,1)} %get-tuple-element.47), channel_id=1, source_target_pairs={{0,1},{1,2},{2,3},{3,4},{4,5},{5,6},{6,7},{7,0},{8,9},{9,10},{10,1... | collective-permute-start | bytes 98312 | tf_op jit(solution)/shard_map/ppermute | solution.py:15
  54.8 0.7 copy-start.35
  56.5 6.7 %collective-permute-start.8 = (bf16[2,32,256]{2,1,0:T(8,128)(2,1)S(1)}, bf16[2,32,256]{2,1,0:T(8,128)(2,1)S(1)}, u32[]{:S(2)}, u32[]{:S(2)}) collective-permute-start(bf16[2,32,256]{2,1,0:T(8,128)(2,1)S(1)} %get-tuple-element.41), channel_id=1, source_target_pairs={{0,1},{1,2},{2,3},{3,4},{4,5},{5,6},{6,7},{7,0},{8,9},{9,10},{10,1... | collective-permute-start | bytes 98312 | tf_op jit(solution)/shard_map/ppermute | solution.py:15
  57.1 0.7 copy-start.31
  58.9 7.7 %copy-start.8 = (f32[128,1024]{1,0:T(8,128)S(1)}, f32[128,1024]{1,0:T(8,128)}, u32[]{:S(2)}) copy-start(f32[128,1024]{1,0:T(8,128)} %copy-done.7) | copy-start | bytes 1572868
  63.1 3.3 %collective-permute-start.9 = (bf16[2,32,256]{2,1,0:T(8,128)(2,1)S(1)}, bf16[2,32,256]{2,1,0:T(8,128)(2,1)S(1)}, u32[]{:S(2)}, u32[]{:S(2)}) collective-permute-start(bf16[2,32,256]{2,1,0:T(8,128)(2,1)S(1)} %fusion.180), channel_id=1, source_target_pairs={{0,8},{8,16},{16,24},{24,0},{1,9},{9,17},{17,25},{25,1},{2,10},{10... | collective-permute-start | bytes 98312 | tf_op jit(solution)/shard_map/ppermute | solution.py:15
  63.2 16.6 %collective-permute-start.5 = (bf16[2,32,256]{2,1,0:T(8,128)(2,1)S(1)}, bf16[2,32,256]{2,1,0:T(8,128)(2,1)S(1)}, u32[]{:S(2)}, u32[]{:S(2)}) collective-permute-start(bf16[2,32,256]{2,1,0:T(8,128)(2,1)S(1)} %fusion.183), channel_id=1, source_target_pairs={{0,8},{8,16},{16,24},{24,0},{1,9},{9,17},{17,25},{25,1},{2,10},{10... | collective-permute-start | bytes 98312 | tf_op jit(solution)/shard_map/ppermute | solution.py:15
  66.5 4.0 %copy-start.5 = (bf16[2,2,32,256]{3,2,1,0:T(8,128)(2,1)}, bf16[2,2,32,256]{3,2,1,0:T(8,128)(2,1)S(1)}, u32[]{:S(2)}) copy-start(bf16[2,2,32,256]{3,2,1,0:T(8,128)(2,1)S(1)} %fusion.166) | copy-start | bytes 196612
  66.5 0.7 copy-start.21
  66.5 0.7 copy-start.26
  69.6 0.7 copy-start.33
  70.5 0.7 copy-start.18
  70.5 2.5 %copy-start.19 = (s32[1,1,3,128]{3,2,1,0:T(4,128)S(1)}, s32[1,1,3,128]{3,2,1,0:T(4,128)}, u32[]{:S(2)}) copy-start(s32[1,1,3,128]{3,2,1,0:T(4,128)} %copy.107) | copy-start | bytes 4612
  75.2 0.8 copy-start.11
  76.4 0.8 copy-start.4
  79.5 0.8 copy-start.10
  80.3 0.7 copy-start.23
  80.3 0.7 copy-start.41
  82.3 0.7 copy-start.43
  83.6 0.8 copy-start.6
  125.3 0.7 copy-start.34
  (12 other events, 7.0 us)
where the time goes:
time: 129 us; the launch traced here: 127 us
  blocking collectives  37.3 us (29%)
  matrix products  35.1 us (27%)
  local copies, waits for them, and re-layouts  22.2 us (17%)
  starting transfers between devices  13 us (10%)
  other arithmetic  9.54 us (7%)
  waiting for transfers between devices  7.58 us (6%)
  between operations  1.87 us (1%)
    psum x1, blocking collectives, on_device(): grad_tables = lax.psum(jnp.stack([table_first, table_second]), ('gx', 'gy'))  37.3 us
    unnamed x103, local copies, waits for them, and re-layouts  15.8 us
    ppermute x10, starting transfers between devices, from_behind(): return lax.ppermute(value, axis, pairs)  13 us
    dot_general x18, matrix products, relative_bias(): jnp.einsum('klu,tu->klt', left_factor, indicator_matrix, precision=highes...  8.74 us
    ppermute x10, waiting for transfers between devices, from_behind(): return lax.ppermute(value, axis, pairs)  7.58 us
    dot_general x18, matrix products, relative_bias(): jnp.einsum('dx,cxq->cdq', indicator_matrix, banded_offset_matrix, precisi...  5.59 us
    dot_general x18, matrix products, relative_bias(): jnp.einsum('hr,abr->hab', bias_table[axis_index], selection_matrix, preci...  4.86 us
    dot_general x4, matrix products, swin_block(): jnp.dot(normed, weight_qkv, preferred_element_type=jnp.float32)  4.2 us
  transfers between devices with their start and end apart: 10, of which 4 were waited for; matrix products, arithmetic and copies ran while one was open for 24% of the time, Pallas kernels for 0%

commit v1 on v0

v1 whole, which is shorter than its diff:
```python
from functools import partial

import jax
import jax.numpy as jnp
from jax import lax
from jax.experimental import pallas as pl
from jax.experimental.pallas import tpu as pltpu
from jax.sharding import PartitionSpec as P

EPSILON = 1e-05
GELU_SCALE = 0.7978845608028654
GELU_CUBE = 0.044715
MESH = pl.DeviceIdType.MESH
F32 = jnp.float32
BF16 = jnp.bfloat16


def dot_nn(a, b):
    return jnp.dot(a, b, preferred_element_type=F32)


def dot_nt(a, b):
    return lax.dot_general(a, b, (((1,), (1,)), ((), ())), preferred_element_type=F32)


def norm_parts(values):
    mean_value = jnp.mean(values, axis=-1, keepdims=True)
    centred = values - mean_value
    variance = jnp.mean(centred * centred, axis=-1, keepdims=True)
    scale = lax.rsqrt(variance + EPSILON)
    return centred * scale, scale


def norm_pullback(cotangent, gain, unit, scale):
    inner = cotangent * gain
    first = jnp.mean(inner, axis=-1, keepdims=True)
    second = jnp.mean(inner * unit, axis=-1, keepdims=True)
    return scale * (inner - first - unit * second)


def split_two(values):
    high = values.astype(BF16)
    return high, (values - high.astype(F32)).astype(BF16)


def kernel(
    nx, ny,
    feat, occ, coords, gains, tables, wqkv, wout, wup, wdown, gout,
    out_points, grad_points, grad_tables,
    x_v, g_v, wqkv_v, wout_v, wup_v, wdown_v,
    meta, meta_recv, g_roll, first, rolled, second, back, grad_mid, grad_first,
    table_pad, band, left_bias, diag, probs, proj, keys_t, unit_one, unit_two,
    rstd_one, rstd_two, gelu_in, onehot_s, onehot_t, score_cot, q_stack, mix_stack,
    t_send, t_recv_x, t_mid, t_recv_y,
    load_sem, send_sem, recv_sem, tx_send, tx_recv, ty_send, ty_recv,
):
    slots, width = x_v.shape
    quarter = slots // 4
    heads = tables.shape[2]
    span = tables.shape[3]
    cells = (span + 1) // 2
    half = cells // 2
    head_size = width // heads
    scale = head_size ** -0.5
    i = lax.axis_index("gx")
    j = lax.axis_index("gy")
    up_i, down_i = lax.rem(i + 1, nx), lax.rem(i + nx - 1, nx)
    up_j, down_j = lax.rem(j + 1, ny), lax.rem(j + ny - 1, ny)

    barrier = pltpu.get_barrier_semaphore()
    for step in range(1, nx):
        pl.semaphore_signal(barrier, 1, device_id=(lax.rem(i + step, nx), j), device_id_type=MESH)
    for step in range(1, ny):
        pl.semaphore_signal(barrier, 1, device_id=(i, lax.rem(j + step, ny)), device_id_type=MESH)
    pl.semaphore_signal(barrier, 1, device_id=(up_i, up_j), device_id_type=MESH)
    pl.semaphore_signal(barrier, 1, device_id=(down_i, down_j), device_id_type=MESH)

    pairs = [(feat.at[0, 0], x_v)]
    for k in range(2):
        pairs += [
            (wqkv.at[k], wqkv_v.at[k]),
            (wout.at[k], wout_v.at[k]),
            (wup.at[k], wup_v.at[k]),
            (wdown.at[k], wdown_v.at[k]),
        ]
    pairs.append((gout.at[0, 0], g_v))
    loads = [pltpu.make_async_copy(a, b, load_sem.at[n]) for n, (a, b) in enumerate(pairs)]
    for load in loads:
        load.start()

    def remote(source, target, place, device):
        return pltpu.make_async_remote_copy(
            src_ref=source, dst_ref=target, send_sem=send_sem.at[place],
            recv_sem=recv_sem.at[place], device_id=device, device_id_type=MESH,
        )

    def rows(number):
        return pl.ds(number * quarter, quarter)

    def roll_forward(source, target, base):
        copies = [
            remote(source.at[rows(0)], target.at[rows(3)], base, (down_i, down_j)),
            remote(source.at[rows(1)], target.at[rows(2)], base + 1, (down_i, j)),
            remote(source.at[rows(2)], target.at[rows(1)], base + 2, (i, down_j)),
        ]
        for copy in copies:
            copy.start()
        target[rows(0)] = source[rows(3)]
        return copies

    def roll_backward(source, target, base):
        copies = [
            remote(source.at[rows(3)], target.at[rows(0)], base, (up_i, up_j)),
            remote(source.at[rows(2)], target.at[rows(1)], base + 1, (up_i, j)),
            remote(source.at[rows(1)], target.at[rows(2)], base + 2, (i, up_j)),
        ]
        for copy in copies:
            copy.start()
        target[rows(3)] = source[rows(0)]
        return copies

    lane = lax.broadcasted_iota(jnp.int32, (heads, slots), 1)
    lane_row = lax.broadcasted_iota(jnp.int32, (1, slots), 1)
    channel = lax.broadcasted_iota(jnp.int32, (1, width), 1)
    head_masks = [
        ((channel >= h * head_size) & (channel < (h + 1) * head_size)).astype(F32).astype(BF16)
        for h in range(heads)
    ]
    pad_rows = 32

    def prepare_bias(k, occupied_row, coord_rows):
        cell = lax.broadcasted_iota(jnp.int32, (cells, slots), 0)
        blocks = [(jnp.broadcast_to(c, (cells, slots)) == cell).astype(F32) for c in coord_rows]
        empty = jnp.zeros((cells, slots), F32)
        first_row = cell == 0
        mask_block = jnp.where(
            first_row, jnp.broadcast_to(occupied_row.astype(F32) - 1.0, (cells, slots)), 0.0
        )
        one_block = jnp.where(first_row, 1.0, 0.0)
        rest = jnp.zeros((slots - 2 * pad_rows, slots), F32)
        right = jnp.concatenate(
            blocks + [one_block] + blocks + [empty, rest], axis=0
        ).astype(BF16)
        left = jnp.concatenate(blocks + [mask_block, empty, empty, empty, empty, rest], axis=0)
        left_t = jnp.transpose(left)
        onehot_s[k] = left_t.astype(BF16)
        onehot_t[k] = jnp.concatenate(blocks + [empty], axis=0).astype(BF16)
        table_pad[...] = jnp.zeros_like(table_pad)
        for e in range(3):
            table_pad[e, :, 0:span] = tables[k, e]
        mask_row = jnp.where(lane == 3 * cells, 1e30, 0.0)
        for u in range(cells):
            row = mask_row if u == 0 else jnp.zeros_like(mask_row)
            band[pl.ds(3 * cells + u, heads, stride=pad_rows), :] = row
        for e in range(3):
            padded = table_pad[e]
            inside = (lane >= e * cells) & (lane < (e + 1) * cells)
            for u in range(cells):
                shift = (e * cells + u - (cells - 1)) % slots
                moved = pltpu.roll(padded, shift, 1) if shift else padded
                tile = jnp.where(inside, moved, 0.0)
                high = tile.astype(BF16).astype(F32)
                tile = high + pltpu.roll(tile - high, pad_rows, 1)
                band[pl.ds(e * cells + u, heads, stride=pad_rows), :] = tile
        left_hot = onehot_s[k][:, 0:pad_rows]
        for h in range(heads):
            banded = band[h * pad_rows:(h + 1) * pad_rows, :].astype(BF16)
            factor = dot_nn(left_hot, banded).astype(BF16)
            left_bias[k, h] = dot_nn(factor, right)
        return left_t[:, 3 * cells:3 * cells + 1] + 1.0

    def attention_part(k, hidden):
        unit, rstd = norm_parts(hidden)
        unit_one[k] = unit
        rstd_one[k] = rstd
        normed = (unit * gains[k, 0:1]).astype(BF16)
        loads[1 + 4 * k].wait()
        projected = dot_nn(normed, wqkv_v[k])
        proj[k] = projected.astype(BF16)
        keys_t[k] = jnp.transpose(projected[:, width:2 * width]).astype(BF16)
        values_t = jnp.transpose(projected[:, 2 * width:]).astype(BF16)
        queries = proj[k, :, 0:width]
        keys = proj[k, :, width:2 * width]
        pieces = []
        for h in range(heads):
            scores = dot_nt(keys * head_masks[h], queries) * scale + left_bias[k, h]
            top = jnp.max(scores, axis=0, keepdims=True)
            powers = jnp.exp(scores - top)
            weights = (powers * (1.0 / jnp.sum(powers, axis=0, keepdims=True))).astype(BF16)
            probs[k, h] = weights
            pieces.append(dot_nn(values_t[h * head_size:(h + 1) * head_size], weights))
        mixed = jnp.transpose(jnp.concatenate(pieces, axis=0)).astype(BF16)
        loads[2 + 4 * k].wait()
        return hidden + dot_nn(mixed, wout_v[k])

    def feed_part(k, middle):
        unit, rstd = norm_parts(middle)
        unit_two[k] = unit
        rstd_two[k] = rstd
        normed = (unit * gains[k, 1:2]).astype(BF16)
        loads[3 + 4 * k].wait()
        wide = dot_nn(normed, wup_v[k])
        gelu_in[k] = wide
        inner = jnp.tanh(GELU_SCALE * (wide + GELU_CUBE * (wide * wide * wide)))
        expanded = (0.5 * wide * (1.0 + inner)).astype(BF16)
        loads[4 + 4 * k].wait()
        return (middle + dot_nn(expanded, wdown_v[k])).astype(BF16)

    def gelu_slope(k):
        wide = gelu_in[k]
        square = wide * wide
        inner = jnp.tanh(GELU_SCALE * (wide + GELU_CUBE * (square * wide)))
        gelu_in[k] = 0.5 * (1.0 + inner) + (0.5 * GELU_SCALE) * wide * (1.0 - inner * inner) * (
            1.0 + (3.0 * GELU_CUBE) * square
        )

    def block_pullback(k, cotangent, with_tables):
        cot_wide = dot_nt(cotangent, wdown_v[k]).astype(BF16).astype(F32) * gelu_in[k]
        cot_normed = dot_nt(cot_wide.astype(BF16), wup_v[k]).astype(BF16).astype(F32)
        cot_middle = cotangent.astype(F32) + norm_pullback(
            cot_normed, gains[k, 1:2], unit_two[k], rstd_two[k]
        )
        cot_mixed = dot_nt(cot_middle.astype(BF16), wout_v[k]).astype(BF16)
        queries = proj[k, :, 0:width]
        values = proj[k, :, 2 * width:]
        hot_twice = jnp.concatenate([onehot_s[k], onehot_s[k]], axis=0)
        hot_t_twice = jnp.concatenate([onehot_t[k], onehot_t[k]], axis=1)
        pieces, tile_list = [], []
        for h in range(heads):
            here = pl.ds(h * slots, slots)
            cot_probs = dot_nt(values * head_masks[h], cot_mixed).astype(BF16).astype(F32)
            weights = probs[k, h].astype(F32)
            product = weights * cot_probs
            total = jnp.sum(product, axis=0, keepdims=True)
            cot_scores = product - weights * total
            high, low = split_two(cot_scores)
            pieces.append(dot_nn(keys_t[k, h * head_size:(h + 1) * head_size], high))
            score_cot[:, here] = high
            q_stack[here, :] = queries * head_masks[h]
            mix_stack[here, :] = cot_mixed * head_masks[h]
            by_key = dot_nn(jnp.concatenate([high, low], axis=1), hot_twice)
            key_high, key_low = split_two(by_key)
            diag[h * pad_rows:(h + 1) * pad_rows, :] = dot_nn(
                hot_t_twice, jnp.concatenate([key_high, key_low], axis=0)
            )
        sums = jnp.zeros((heads, slots), F32)
        for e in range(3):
            inside = (lane >= e * cells) & (lane < (e + 1) * cells)
            for u in range(cells):
                tile = jnp.where(inside, diag[pl.ds(e * cells + u, heads, stride=pad_rows), :], 0.0)
                shift = e * cells + (cells - 1) - u
                sums = sums + (pltpu.roll(tile, shift, 1) if shift else tile)
        t_send[k * heads:(k + 1) * heads, :] = sums
        with_tables()
        cot_queries = (jnp.transpose(jnp.concatenate(pieces, axis=0)) * scale).astype(BF16)
        cot_keys = (dot_nn(score_cot[...], q_stack[...]) * scale).astype(BF16)
        probs_wide = jnp.concatenate([probs[k, h] for h in range(heads)], axis=1)
        cot_values = dot_nn(probs_wide, mix_stack[...]).astype(BF16)
        cot_proj = jnp.concatenate([cot_queries, cot_keys, cot_values], axis=1)
        cot_normed = dot_nt(cot_proj, wqkv_v[k]).astype(BF16).astype(F32)
        return (
            cot_middle + norm_pullback(cot_normed, gains[k, 0:1], unit_one[k], rstd_one[k])
        ).astype(BF16)

    meta[...] = jnp.zeros_like(meta)
    meta[0:1, :] = occ[0]
    meta[1:4, :] = coords[0, 0]
    occupied = prepare_bias(0, occ[0], [coords[0, 0, e:e + 1] for e in range(3)])
    loads[0].wait()
    middle = attention_part(0, x_v[...].astype(F32))

    pl.semaphore_wait(barrier, nx + ny)
    meta_copies = [
        remote(meta, meta_recv.at[0], 0, (down_i, down_j)),
        remote(meta, meta_recv.at[1], 1, (down_i, j)),
        remote(meta, meta_recv.at[2], 2, (i, down_j)),
    ]
    for copy in meta_copies:
        copy.start()
    loads[9].wait()
    grad_copies = roll_forward(g_v, g_roll, 3)

    first[...] = feed_part(0, middle)
    first_copies = roll_forward(first, rolled, 6)

    for copy in meta_copies:
        copy.wait()
    own = pltpu.roll(meta[...], quarter, 1)
    from_y = pltpu.roll(meta_recv[2], slots - quarter, 1)
    from_x = pltpu.roll(meta_recv[1], quarter, 1)
    from_xy = pltpu.roll(meta_recv[0], slots - quarter, 1)
    moved = jnp.where(
        lane_row < quarter, own,
        jnp.where(lane_row < 2 * quarter, from_y, jnp.where(lane_row < 3 * quarter, from_x, from_xy)),
    )

    def wrapped(values):
        moved_on = values + half
        return jnp.where(moved_on >= cells, moved_on - cells, moved_on)

    shifted_occupied = prepare_bias(
        1, moved[0:1], [wrapped(moved[1:2]), wrapped(moved[2:3]), moved[3:4]]
    )
    gelu_slope(0)
    for copy in first_copies:
        copy.wait()
    middle = attention_part(1, rolled[...].astype(F32))
    second[...] = feed_part(1, middle)
    second_copies = roll_backward(second, back, 9)
    gelu_slope(1)
    for copy in grad_copies:
        copy.wait()
    grad_in = (g_roll[...].astype(F32) * shifted_occupied).astype(BF16)
    grad_mid[...] = block_pullback(1, grad_in, lambda: None)
    mid_copies = roll_backward(grad_mid, grad_first, 12)
    for copy in second_copies:
        copy.wait()
    out_points[0, 0] = (back[...].astype(F32) * occupied).astype(BF16)
    for copy in mid_copies:
        copy.wait()

    def exchange(source, target, send, recv, me, count, device_of):
        copies = []
        for step in range(1, count):
            copies.append(
                pltpu.make_async_remote_copy(
                    src_ref=source, dst_ref=target.at[me], send_sem=send.at[step],
                    recv_sem=recv.at[step], device_id=device_of(lax.rem(me + step, count)),
                    device_id_type=MESH,
                )
            )
            copies[-1].start()
        target[me] = source[...]
        return copies

    table_copies = []

    def send_tables():
        table_copies.extend(
            exchange(t_send, t_recv_x, tx_send, tx_recv, i, nx, lambda other: (other, j))
        )

    grad_points[0, 0] = block_pullback(0, grad_first[...], send_tables)
    for copy in table_copies:
        copy.wait()
    total = t_recv_x[0]
    for n in range(1, nx):
        total = total + t_recv_x[n]
    t_mid[...] = total
    for copy in exchange(t_mid, t_recv_y, ty_send, ty_recv, j, ny, lambda other: (i, other)):
        copy.wait()
    total = t_recv_y[0]
    for n in range(1, ny):
        total = total + t_recv_y[n]
    for k in range(2):
        for e in range(3):
            tile = total[k * heads:(k + 1) * heads]
            shift = (slots - 2 * cells * e) % slots
            tile = pltpu.roll(tile, shift, 1) if shift else tile
            grad_tables[k, e] = tile[:, 0:span]


def on_device(
    nx, ny, features, occupancy, coords, norm_gains, bias_tables, w_qkv, w_out, w_up, w_down, grad_out
):
    slots, width = features.shape[2:]
    heads = bias_tables.shape[2]
    hidden = w_up.shape[2]
    points = (slots, width)
    vmem = pl.BlockSpec(memory_space=pltpu.VMEM)
    hbm = pl.BlockSpec(memory_space=pl.ANY)
    dma = pltpu.SemaphoreType.DMA
    scratch = [
        pltpu.VMEM(points, BF16),
        pltpu.VMEM(points, BF16),
        pltpu.VMEM(w_qkv.shape, BF16),
        pltpu.VMEM(w_out.shape, BF16),
        pltpu.VMEM(w_up.shape, BF16),
        pltpu.VMEM(w_down.shape, BF16),
        pltpu.VMEM((8, slots), jnp.int32),
        pltpu.VMEM((3, 8, slots), jnp.int32),
    ]
    scratch += [pltpu.VMEM(points, BF16) for _ in range(7)]
    scratch += [
        pltpu.VMEM((3, heads, slots), F32),
        pltpu.VMEM((heads * 32, slots), F32),
        pltpu.VMEM((2, heads, slots, slots), F32),
        pltpu.VMEM((heads * 32, slots), F32),
        pltpu.VMEM((2, heads, slots, slots), BF16),
        pltpu.VMEM((2, slots, 3 * width), BF16),
        pltpu.VMEM((2, width, slots), BF16),
        pltpu.VMEM((2,) + points, F32),
        pltpu.VMEM((2,) + points, F32),
        pltpu.VMEM((2, slots, 1), F32),
        pltpu.VMEM((2, slots, 1), F32),
        pltpu.VMEM((2, slots, hidden), F32),
        pltpu.VMEM((2, slots, slots), BF16),
        pltpu.VMEM((2, 32, slots), BF16),
        pltpu.VMEM((slots, heads * slots), BF16),
        pltpu.VMEM((heads * slots, width), BF16),
        pltpu.VMEM((heads * slots, width), BF16),
        pltpu.VMEM((2 * heads, slots), F32),
        pltpu.VMEM((nx, 2 * heads, slots), F32),
        pltpu.VMEM((2 * heads, slots), F32),
        pltpu.VMEM((ny, 2 * heads, slots), F32),
        dma((10,)), dma((15,)), dma((15,)), dma((nx,)), dma((nx,)), dma((ny,)), dma((ny,)),
    ]
    return pl.pallas_call(
        partial(kernel, nx, ny),
        out_shape=(
            jax.ShapeDtypeStruct(features.shape, BF16),
            jax.ShapeDtypeStruct(features.shape, BF16),
            jax.ShapeDtypeStruct(bias_tables.shape, F32),
        ),
        in_specs=[hbm, vmem, vmem, vmem, vmem, hbm, hbm, hbm, hbm, hbm],
        out_specs=(vmem, vmem, vmem),
        scratch_shapes=scratch,
        compiler_params=pltpu.CompilerParams(
            collective_id=0, has_side_effects=True, vmem_limit_bytes=60 * 1024 * 1024
        ),
    )(features, occupancy, coords, norm_gains, bias_tables, w_qkv, w_out, w_up, w_down, grad_out)


def solution(mesh):
    spread = P("gx", "gy", None, None)
    return jax.shard_map(
        partial(on_device, mesh.shape["gx"], mesh.shape["gy"]),
        mesh=mesh,
        in_specs=(spread, P("gx", "gy", None), spread, P(), P(), P(), P(), P(), P(), spread),
        out_specs=(spread, spread, P()),
        check_vma=False,
    )
```

time: 129 us -> 37.1 us (0.29); the launches traced: 127 us -> 36.8 us
  blocking collectives: 37.3 us -> 0 us
  matrix products: 35.1 us -> 0 us
  Pallas kernels: 0 us -> 32.1 us
  local copies, waits for them, and re-layouts: 22.2 us -> 4.11 us
  starting transfers between devices: 13 us -> 0 us
  other arithmetic: 9.54 us -> 0 us
  waiting for transfers between devices: 7.58 us -> 0 us
    psum x1 -> x0, blocking collectives: 37.3 us -> none  [on_device(): grad_tables = lax.psum(jnp.stack([table_first, table_second]), ('gx', 'gy'))]
    dot_general x82 -> x0, matrix products: 35.1 us -> none  [the longest x18 8.74 us: relative_bias(): jnp.einsum('klu,tu->klt', left_factor, indicator_matrix, precision=highes...]
    pallas_call x0 -> x1, Pallas kernels: none -> 32.1 us  [on_device(): pl.pallas_call(partial(kernel, nx, ny), out_shape=(jax.ShapeDtypeStruct(f...]
    ppermute x10 -> x0, starting transfers between devices: 13 us -> none  [from_behind(): return lax.ppermute(value, axis, pairs)]
    unnamed x103 -> x8, local copies, waits for them, and re-layouts: 15.8 us -> 4.11 us
    ppermute x10 -> x0, waiting for transfers between devices: 7.58 us -> none  [from_behind(): return lax.ppermute(value, axis, pairs)]
    convert_element_type x5 -> x0, other arithmetic: 2.79 us -> none  [the longest x1 1.99 us: on_device(): occupied = occupancy[0, 0].astype(jnp.float32)]
    squeeze x5 -> x0, local copies, waits for them, and re-layouts: 2.67 us -> none  [the longest x2 1.42 us: roll_half(): upper_half = lax.index_in_dim(array, 1, position, keepdims=False)]
  transfers between devices with their start and end apart: 10 -> 0, of which waited for: 4 -> 0; matrix products, arithmetic and copies ran while one was open for 24% -> 0% of each run, Pallas kernels for 0% -> 0%
where the time goes in v1:
time: 37.1 us; the launch traced here: 36.8 us
  Pallas kernels  32.1 us (87%)
  local copies, waits for them, and re-layouts  4.11 us (11%)
  between operations  0.65 us (2%)
    pallas_call x1, Pallas kernels, on_device(): pl.pallas_call(partial(kernel, nx, ny), out_shape=(jax.ShapeDtypeStruct(f...  32.1 us
    unnamed x8, local copies, waits for them, and re-layouts  4.11 us

profile of v1, /device:TPU:0, one launch (start us, length us, event | category | flops | bytes accessed | tf_op | source)
XLA Modules:
  0.0 36.8 jit_solution(3451547315613543763)
XLA Ops:
  0.6 1.3 %copy.13.coords = s32[1,1,3,128]{3,2,1,0:T(4,128)} copy(s32[1,1,3,128]{3,1,2,0:T(1,128)} %param.12) | data formatting | bytes 3072 | tf_op args[2]
  1.9 32.1 %shard_map.121 = (bf16[1,1,128,256]{3,2,1,0:T(8,128)(2,1)}, bf16[1,1,128,256]{3,2,1,0:T(8,128)(2,1)}, f32[2,3,8,15]{3,2,1,0:T(8,128)}) custom-call(bf16[1,1,128,256]{3,2,1,0:T(8,128)(2,1)} %feat.1, s32[1,1,128]{2,1,0:T(1,128)} %occ.1, s32[1,1,3,128]{3,2,1,0:T(4,128)} %copy.13.coords, f32[2,2,256]{2,1,0:T(2,128)} %gains.1, f32[2,3,8,15]{3,2,1,0:T(8,128)} %tables.1, ...), custom_call_target="tpu_custom_call" | custom-call | tf_op jit(solution)/shard_map/pallas_call | solution.py:408
  34.0 0.0 copy-start
  34.0 1.5 %copy.17 = bf16[1,1,128,256]{3,2,1,0:T(8,128)(2,1)} copy(bf16[1,1,128,256]{3,2,1,0:T(8,128)(2,1)} %get-tuple-element.6) | data formatting | bytes 131072
  35.5 0.0 copy-done
  35.5 0.0 copy-start.1
  35.5 0.6 %copy.18 = bf16[1,1,128,256]{3,2,1,0:T(8,128)(2,1)} copy(bf16[1,1,128,256]{3,2,1,0:T(8,128)(2,1)S(1)} %copy-done) | data formatting | bytes 131072
  36.1 0.1 copy-done.1
  36.2 0.6 %copy.19 = f32[2,3,8,15]{3,2,1,0:T(8,128)} copy(f32[2,3,8,15]{3,2,1,0:T(8,128)S(1)} %copy-done.1) | data formatting | bytes 5760
Async XLA Ops:
  34.0 1.5 %copy-start = (bf16[1,1,128,256]{3,2,1,0:T(8,128)(2,1)S(1)}, bf16[1,1,128,256]{3,2,1,0:T(8,128)(2,1)}, u32[]{:S(2)}) copy-start(bf16[1,1,128,256]{3,2,1,0:T(8,128)(2,1)} %get-tuple-element.7) | copy-start | bytes 196612
  35.5 0.7 %copy-start.1 = (f32[2,3,8,15]{3,2,1,0:T(8,128)S(1)}, f32[2,3,8,15]{3,2,1,0:T(8,128)}, u32[]{:S(2)}) copy-start(f32[2,3,8,15]{3,2,1,0:T(8,128)} %get-tuple-element.8) | copy-start | bytes 8644

commit v2 on v1

--- a/solution.py
+++ b/solution.py
@@ -10,6 +10,7 @@
 EPSILON = 1e-05
 GELU_SCALE = 0.7978845608028654
 GELU_CUBE = 0.044715
+VMEM_BYTES = 67_043_328
 MESH = pl.DeviceIdType.MESH
 F32 = jnp.float32
 BF16 = jnp.bfloat16
@@ -45,12 +46,14 @@
 
 def kernel(
     nx, ny,
-    feat, occ, coords, gains, tables, wqkv, wout, wup, wdown, gout,
+    feat, occ_h, coords_h, gains_h, tables_h, wqkv, wout, wup, wdown, gout,
     out_points, grad_points, grad_tables,
+    occ, coords, gains, tables,
     x_v, g_v, wqkv_v, wout_v, wup_v, wdown_v,
     meta, meta_recv, g_roll, first, rolled, second, back, grad_mid, grad_first,
     table_pad, band, left_bias, diag, probs, proj, keys_t, unit_one, unit_two,
-    rstd_one, rstd_two, gelu_in, onehot_s, onehot_t, score_cot, q_stack, mix_stack,
+    rstd_one, rstd_two, gelu_in, expanded_v, cot_wide_v, onehot_s, onehot_t, score_cot, cot_pair,
+    q_stack, mix_stack,
     t_send, t_recv_x, t_mid, t_recv_y,
     load_sem, send_sem, recv_sem, tx_send, tx_recv, ty_send, ty_recv,
 ):
@@ -67,14 +70,6 @@
     up_i, down_i = lax.rem(i + 1, nx), lax.rem(i + nx - 1, nx)
     up_j, down_j = lax.rem(j + 1, ny), lax.rem(j + ny - 1, ny)
 
-    barrier = pltpu.get_barrier_semaphore()
-    for step in range(1, nx):
-        pl.semaphore_signal(barrier, 1, device_id=(lax.rem(i + step, nx), j), device_id_type=MESH)
-    for step in range(1, ny):
-        pl.semaphore_signal(barrier, 1, device_id=(i, lax.rem(j + step, ny)), device_id_type=MESH)
-    pl.semaphore_signal(barrier, 1, device_id=(up_i, up_j), device_id_type=MESH)
-    pl.semaphore_signal(barrier, 1, device_id=(down_i, down_j), device_id_type=MESH)
-
     pairs = [(feat.at[0, 0], x_v)]
     for k in range(2):
         pairs += [
@@ -84,9 +79,18 @@
             (wdown.at[k], wdown_v.at[k]),
         ]
     pairs.append((gout.at[0, 0], g_v))
+    pairs += [(occ_h, occ), (coords_h, coords), (gains_h, gains), (tables_h, tables)]
     loads = [pltpu.make_async_copy(a, b, load_sem.at[n]) for n, (a, b) in enumerate(pairs)]
-    for load in loads:
-        load.start()
+    for n in (10, 11, 12, 13, *range(10)):
+        loads[n].start()
+
+    barrier = pltpu.get_barrier_semaphore()
+    for step in range(1, nx):
+        pl.semaphore_signal(barrier, 1, device_id=(lax.rem(i + step, nx), j), device_id_type=MESH)
+    for step in range(1, ny):
+        pl.semaphore_signal(barrier, 1, device_id=(i, lax.rem(j + step, ny)), device_id_type=MESH)
+    pl.semaphore_signal(barrier, 1, device_id=(up_i, up_j), device_id_type=MESH)
+    pl.semaphore_signal(barrier, 1, device_id=(down_i, down_j), device_id_type=MESH)
 
     def remote(source, target, place, device):
         return pltpu.make_async_remote_copy(
@@ -163,13 +167,20 @@
                 tile = high + pltpu.roll(tile - high, pad_rows, 1)
                 band[pl.ds(e * cells + u, heads, stride=pad_rows), :] = tile
         left_hot = onehot_s[k][:, 0:pad_rows]
-        for h in range(heads):
-            banded = band[h * pad_rows:(h + 1) * pad_rows, :].astype(BF16)
-            factor = dot_nn(left_hot, banded).astype(BF16)
-            left_bias[k, h] = dot_nn(factor, right)
+        banded = jnp.concatenate(
+            [band[h * pad_rows:(h + 1) * pad_rows, :] for h in range(heads)], axis=1
+        ).astype(BF16)
+        factors = dot_nn(left_hot, banded).astype(BF16)
+        factors = jnp.concatenate(
+            [factors[:, h * slots:(h + 1) * slots] for h in range(heads)], axis=0
+        )
+        left_bias[k] = dot_nn(factors, right)
         return left_t[:, 3 * cells:3 * cells + 1] + 1.0
 
-    def attention_part(k, hidden):
+    def stacked(values):
+        return jnp.concatenate([values * head_masks[h] for h in range(heads)], axis=0)
+
+    def attention_head(k, hidden):
         unit, rstd = norm_parts(hidden)
         unit_one[k] = unit
         rstd_one[k] = rstd
@@ -178,96 +189,150 @@
         projected = dot_nn(normed, wqkv_v[k])
         proj[k] = projected.astype(BF16)
         keys_t[k] = jnp.transpose(projected[:, width:2 * width]).astype(BF16)
-        values_t = jnp.transpose(projected[:, 2 * width:]).astype(BF16)
+        return jnp.transpose(projected[:, 2 * width:]).astype(BF16)
+
+    def attention_part(k, hidden, values_t):
         queries = proj[k, :, 0:width]
         keys = proj[k, :, width:2 * width]
+        scores_all = dot_nt(stacked(keys), queries)
         pieces = []
         for h in range(heads):
-            scores = dot_nt(keys * head_masks[h], queries) * scale + left_bias[k, h]
+            here = slice(h * slots, (h + 1) * slots)
+            scores = scores_all[here] * scale + left_bias[k, here]
             top = jnp.max(scores, axis=0, keepdims=True)
             powers = jnp.exp(scores - top)
             weights = (powers * (1.0 / jnp.sum(powers, axis=0, keepdims=True))).astype(BF16)
-            probs[k, h] = weights
+            probs[k, here] = weights
             pieces.append(dot_nn(values_t[h * head_size:(h + 1) * head_size], weights))
         mixed = jnp.transpose(jnp.concatenate(pieces, axis=0)).astype(BF16)
         loads[2 + 4 * k].wait()
         return hidden + dot_nn(mixed, wout_v[k])
 
-    def feed_part(k, middle):
+    hidden_width = wup_v.shape[2]
+    chunk = 2 * slots
+    chunks = [pl.ds(start, chunk) for start in range(0, hidden_width, chunk)]
+
+    def feed_part(k, middle, with_slope):
         unit, rstd = norm_parts(middle)
         unit_two[k] = unit
         rstd_two[k] = rstd
         normed = (unit * gains[k, 1:2]).astype(BF16)
         loads[3 + 4 * k].wait()
-        wide = dot_nn(normed, wup_v[k])
-        gelu_in[k] = wide
-        inner = jnp.tanh(GELU_SCALE * (wide + GELU_CUBE * (wide * wide * wide)))
-        expanded = (0.5 * wide * (1.0 + inner)).astype(BF16)
+        for cut in chunks:
+            wide = dot_nn(normed, wup_v[k, :, cut])
+            square = wide * wide
+            inner = jnp.tanh(wide * (GELU_SCALE + (GELU_SCALE * GELU_CUBE) * square))
+            grown = 0.5 * (1.0 + inner)
+            expanded_v[k, :, cut] = (wide * grown).astype(BF16)
+            if with_slope:
+                gelu_in[k, :, cut] = grown + wide * (0.5 * (1.0 - inner * inner)) * (
+                    GELU_SCALE + (3.0 * GELU_SCALE * GELU_CUBE) * square
+                )
+            else:
+                gelu_in[k, :, cut] = wide
+
+    def feed_out(k, middle):
         loads[4 + 4 * k].wait()
-        return (middle + dot_nn(expanded, wdown_v[k])).astype(BF16)
+        return (middle + dot_nn(expanded_v[k], wdown_v[k])).astype(BF16)
 
     def gelu_slope(k):
-        wide = gelu_in[k]
-        square = wide * wide
-        inner = jnp.tanh(GELU_SCALE * (wide + GELU_CUBE * (square * wide)))
-        gelu_in[k] = 0.5 * (1.0 + inner) + (0.5 * GELU_SCALE) * wide * (1.0 - inner * inner) * (
-            1.0 + (3.0 * GELU_CUBE) * square
-        )
-
-    def block_pullback(k, cotangent, with_tables):
-        cot_wide = dot_nt(cotangent, wdown_v[k]).astype(BF16).astype(F32) * gelu_in[k]
-        cot_normed = dot_nt(cot_wide.astype(BF16), wup_v[k]).astype(BF16).astype(F32)
+        for cut in chunks:
+            wide = gelu_in[k, :, cut]
+            square = wide * wide
+            inner = jnp.tanh(wide * (GELU_SCALE + (GELU_SCALE * GELU_CUBE) * square))
+            gelu_in[k, :, cut] = 0.5 * (1.0 + inner) + wide * (0.5 * (1.0 - inner * inner)) * (
+                GELU_SCALE + (3.0 * GELU_SCALE * GELU_CUBE) * square
+            )
+
+    def pull_wide(k, cotangent):
+        for cut in chunks:
+            cot_wide_v[k, :, cut] = dot_nt(cotangent, wdown_v[k, cut, :]).astype(BF16)
+
+    def pull_scores(k, cotangent):
+        for cut in chunks:
+            cot_wide_v[k, :, cut] = (
+                cot_wide_v[k, :, cut].astype(F32) * gelu_in[k, :, cut]
+            ).astype(BF16)
+        cot_normed = dot_nt(cot_wide_v[k], wup_v[k]).astype(BF16).astype(F32)
         cot_middle = cotangent.astype(F32) + norm_pullback(
             cot_normed, gains[k, 1:2], unit_two[k], rstd_two[k]
         )
         cot_mixed = dot_nt(cot_middle.astype(BF16), wout_v[k]).astype(BF16)
-        queries = proj[k, :, 0:width]
-        values = proj[k, :, 2 * width:]
+        mix_stack[...] = stacked(cot_mixed)
+        cot_all = dot_nt(stacked(proj[k, :, 2 * width:]), cot_mixed)
+        for h in range(heads):
+            here = slice(h * slots, (h + 1) * slots)
+            cot_probs = cot_all[here].astype(BF16).astype(F32)
+            weights = probs[k, here].astype(F32)
+            product = weights * cot_probs
+            total = jnp.sum(product, axis=0, keepdims=True)
+            high, low = split_two(product - weights * total)
+            cot_pair[here, 0:slots] = high
+            cot_pair[here, slots:2 * slots] = low
+        return cot_middle
+
+    def table_sums(k):
         hot_twice = jnp.concatenate([onehot_s[k], onehot_s[k]], axis=0)
         hot_t_twice = jnp.concatenate([onehot_t[k], onehot_t[k]], axis=1)
-        pieces, tile_list = [], []
+        by_key = dot_nn(cot_pair[...], hot_twice)
+        key_high, key_low = split_two(by_key)
+        pair = jnp.concatenate(
+            [
+                jnp.concatenate(
+                    [part[h * slots:(h + 1) * slots] for h in range(heads)], axis=1
+                )
+                for part in (key_high, key_low)
+            ],
+            axis=0,
+        )
+        pairs_sum = dot_nn(hot_t_twice, pair)
         for h in range(heads):
-            here = pl.ds(h * slots, slots)
-            cot_probs = dot_nt(values * head_masks[h], cot_mixed).astype(BF16).astype(F32)
-            weights = probs[k, h].astype(F32)
-            product = weights * cot_probs
-            total = jnp.sum(product, axis=0, keepdims=True)
-            cot_scores = product - weights * total
-            high, low = split_two(cot_scores)
-            pieces.append(dot_nn(keys_t[k, h * head_size:(h + 1) * head_size], high))
-            score_cot[:, here] = high
-            q_stack[here, :] = queries * head_masks[h]
-            mix_stack[here, :] = cot_mixed * head_masks[h]
-            by_key = dot_nn(jnp.concatenate([high, low], axis=1), hot_twice)
-            key_high, key_low = split_two(by_key)
-            diag[h * pad_rows:(h + 1) * pad_rows, :] = dot_nn(
-                hot_t_twice, jnp.concatenate([key_high, key_low], axis=0)
-            )
-        sums = jnp.zeros((heads, slots), F32)
+            diag[h * pad_rows:(h + 1) * pad_rows, :] = pairs_sum[:, h * slots:(h + 1) * slots]
+        sums = []
         for e in range(3):
             inside = (lane >= e * cells) & (lane < (e + 1) * cells)
             for u in range(cells):
                 tile = jnp.where(inside, diag[pl.ds(e * cells + u, heads, stride=pad_rows), :], 0.0)
                 shift = e * cells + (cells - 1) - u
-                sums = sums + (pltpu.roll(tile, shift, 1) if shift else tile)
-        t_send[k * heads:(k + 1) * heads, :] = sums
-        with_tables()
+                sums.append(pltpu.roll(tile, shift, 1) if shift else tile)
+        while len(sums) > 1:
+            sums = [a + b for a, b in zip(sums[0::2], sums[1::2])] + (
+                [sums[-1]] if len(sums) % 2 else []
+            )
+        t_send[k * heads:(k + 1) * heads, :] = sums[0]
+
+    def pull_proj(k):
+        pieces = []
+        for h in range(heads):
+            high = cot_pair[h * slots:(h + 1) * slots, 0:slots]
+            score_cot[:, h * slots:(h + 1) * slots] = high
+            pieces.append(dot_nn(keys_t[k, h * head_size:(h + 1) * head_size], high))
+        q_stack[...] = stacked(proj[k, :, 0:width])
         cot_queries = (jnp.transpose(jnp.concatenate(pieces, axis=0)) * scale).astype(BF16)
         cot_keys = (dot_nn(score_cot[...], q_stack[...]) * scale).astype(BF16)
-        probs_wide = jnp.concatenate([probs[k, h] for h in range(heads)], axis=1)
+        probs_wide = jnp.concatenate(
+            [probs[k, h * slots:(h + 1) * slots] for h in range(heads)], axis=1
+        )
         cot_values = dot_nn(probs_wide, mix_stack[...]).astype(BF16)
-        cot_proj = jnp.concatenate([cot_queries, cot_keys, cot_values], axis=1)
+        return jnp.concatenate([cot_queries, cot_keys, cot_values], axis=1)
+
+    def pull_input(k, cot_proj, cot_middle):
         cot_normed = dot_nt(cot_proj, wqkv_v[k]).astype(BF16).astype(F32)
         return (
             cot_middle + norm_pullback(cot_normed, gains[k, 0:1], unit_one[k], rstd_one[k])
         ).astype(BF16)
 
+    for n in (10, 11, 12, 13):
+        loads[n].wait()
     meta[...] = jnp.zeros_like(meta)
     meta[0:1, :] = occ[0]
-    meta[1:4, :] = coords[0, 0]
-    occupied = prepare_bias(0, occ[0], [coords[0, 0, e:e + 1] for e in range(3)])
+    for e in range(3):
+        meta[e + 1:e + 2, :] = coords[0, e]
     loads[0].wait()
-    middle = attention_part(0, x_v[...].astype(F32))
+    hidden = x_v[...].astype(F32)
+    values_t = attention_head(0, hidden)
+    occupied = prepare_bias(0, occ[0], [coords[0, e] for e in range(3)])
+    middle = attention_part(0, hidden, values_t)
 
     pl.semaphore_wait(barrier, nx + ny)
     meta_copies = [
@@ -280,7 +345,8 @@
     loads[9].wait()
     grad_copies = roll_forward(g_v, g_roll, 3)
 
-    first[...] = feed_part(0, middle)
+    feed_part(0, middle, False)
+    first[...] = feed_out(0, middle)
     first_copies = roll_forward(first, rolled, 6)
 
     for copy in meta_copies:
@@ -302,20 +368,22 @@
         1, moved[0:1], [wrapped(moved[1:2]), wrapped(moved[2:3]), moved[3:4]]
     )
     gelu_slope(0)
+    for copy in grad_copies:
+        copy.wait()
+    grad_in = (g_roll[...].astype(F32) * shifted_occupied).astype(BF16)
+    loads[8].wait()
+    pull_wide(1, grad_in)
     for copy in first_copies:
         copy.wait()
-    middle = attention_part(1, rolled[...].astype(F32))
-    second[...] = feed_part(1, middle)
+    hidden = rolled[...].astype(F32)
+    middle = attention_part(1, hidden, attention_head(1, hidden))
+    feed_part(1, middle, True)
+    cot_middle = pull_scores(1, grad_in)
+    grad_mid[...] = pull_input(1, pull_proj(1), cot_middle)
+    mid_copies = roll_backward(grad_mid, grad_first, 12)
+    second[...] = (middle + dot_nn(expanded_v[1], wdown_v[1])).astype(BF16)
     second_copies = roll_backward(second, back, 9)
-    gelu_slope(1)
-    for copy in grad_copies:
-        copy.wait()
-    grad_in = (g_roll[...].astype(F32) * shifted_occupied).astype(BF16)
-    grad_mid[...] = block_pullback(1, grad_in, lambda: None)
-    mid_copies = roll_backward(grad_mid, grad_first, 12)
-    for copy in second_copies:
-        copy.wait()
-    out_points[0, 0] = (back[...].astype(F32) * occupied).astype(BF16)
+    table_sums(1)
     for copy in mid_copies:
         copy.wait()
 
@@ -333,21 +401,24 @@
         target[me] = source[...]
         return copies
 
-    table_copies = []
-
-    def send_tables():
-        table_copies.extend(
-            exchange(t_send, t_recv_x, tx_send, tx_recv, i, nx, lambda other: (other, j))
-        )
-
-    grad_points[0, 0] = block_pullback(0, grad_first[...], send_tables)
+    cotangent = grad_first[...]
+    pull_wide(0, cotangent)
+    cot_middle = pull_scores(0, cotangent)
+    table_sums(0)
+    table_copies = exchange(t_send, t_recv_x, tx_send, tx_recv, i, nx, lambda other: (other, j))
+    cot_proj = pull_proj(0)
     for copy in table_copies:
         copy.wait()
     total = t_recv_x[0]
     for n in range(1, nx):
         total = total + t_recv_x[n]
     t_mid[...] = total
-    for copy in exchange(t_mid, t_recv_y, ty_send, ty_recv, j, ny, lambda other: (i, other)):
+    table_copies = exchange(t_mid, t_recv_y, ty_send, ty_recv, j, ny, lambda other: (i, other))
+    grad_points[0, 0] = pull_input(0, cot_proj, cot_middle)
+    for copy in second_copies:
+        copy.wait()
+    out_points[0, 0] = (back[...].astype(F32) * occupied).astype(BF16)
+    for copy in table_copies:
         copy.wait()
     total = t_recv_y[0]
     for n in range(1, ny):
@@ -360,17 +431,28 @@
             grad_tables[k, e] = tile[:, 0:span]
 
 
+def finish(points_in, grads_in, tables_in, points_out, grads_out, tables_out):
+    points_out[...] = points_in[...]
+    grads_out[...] = grads_in[...]
+    tables_out[...] = tables_in[...]
+
+
 def on_device(
     nx, ny, features, occupancy, coords, norm_gains, bias_tables, w_qkv, w_out, w_up, w_down, grad_out
 ):
     slots, width = features.shape[2:]
+    coords = jnp.transpose(coords, (0, 2, 1, 3))
     heads = bias_tables.shape[2]
     hidden = w_up.shape[2]
     points = (slots, width)
     vmem = pl.BlockSpec(memory_space=pltpu.VMEM)
-    hbm = pl.BlockSpec(memory_space=pl.ANY)
+    hbm = pl.BlockSpec(memory_space=pltpu.HBM)
     dma = pltpu.SemaphoreType.DMA
     scratch = [
+        pltpu.VMEM(occupancy.shape, jnp.int32),
+        pltpu.VMEM(coords.shape, jnp.int32),
+        pltpu.VMEM(norm_gains.shape, F32),
+        pltpu.VMEM(bias_tables.shape, F32),
         pltpu.VMEM(points, BF16),
         pltpu.VMEM(points, BF16),
         pltpu.VMEM(w_qkv.shape, BF16),
@@ -384,9 +466,9 @@
     scratch += [
         pltpu.VMEM((3, heads, slots), F32),
         pltpu.VMEM((heads * 32, slots), F32),
-        pltpu.VMEM((2, heads, slots, slots), F32),
+        pltpu.VMEM((2, heads * slots, slots), F32),
         pltpu.VMEM((heads * 32, slots), F32),
-        pltpu.VMEM((2, heads, slots, slots), BF16),
+        pltpu.VMEM((2, heads * slots, slots), BF16),
         pltpu.VMEM((2, slots, 3 * width), BF16),
         pltpu.VMEM((2, width, slots), BF16),
         pltpu.VMEM((2,) + points, F32),
@@ -394,31 +476,40 @@
         pltpu.VMEM((2, slots, 1), F32),
         pltpu.VMEM((2, slots, 1), F32),
         pltpu.VMEM((2, slots, hidden), F32),
+        pltpu.VMEM((2, slots, hidden), BF16),
+        pltpu.VMEM((2, slots, hidden), BF16),
         pltpu.VMEM((2, slots, slots), BF16),
         pltpu.VMEM((2, 32, slots), BF16),
         pltpu.VMEM((slots, heads * slots), BF16),
+        pltpu.VMEM((heads * slots, 2 * slots), BF16),
         pltpu.VMEM((heads * slots, width), BF16),
         pltpu.VMEM((heads * slots, width), BF16),
         pltpu.VMEM((2 * heads, slots), F32),
         pltpu.VMEM((nx, 2 * heads, slots), F32),
         pltpu.VMEM((2 * heads, slots), F32),
         pltpu.VMEM((ny, 2 * heads, slots), F32),
-        dma((10,)), dma((15,)), dma((15,)), dma((nx,)), dma((nx,)), dma((ny,)), dma((ny,)),
+        dma((14,)), dma((15,)), dma((15,)), dma((nx,)), dma((nx,)), dma((ny,)), dma((ny,)),
     ]
-    return pl.pallas_call(
+    shapes = [(features.shape, BF16), (features.shape, BF16), (bias_tables.shape, F32)]
+    padded_tables = 6 * 8 * slots * 4 * pl.cdiv(heads, 8)
+    room = VMEM_BYTES - 4 * slots * width - padded_tables
+    results = pl.pallas_call(
         partial(kernel, nx, ny),
-        out_shape=(
-            jax.ShapeDtypeStruct(features.shape, BF16),
-            jax.ShapeDtypeStruct(features.shape, BF16),
-            jax.ShapeDtypeStruct(bias_tables.shape, F32),
-        ),
-        in_specs=[hbm, vmem, vmem, vmem, vmem, hbm, hbm, hbm, hbm, hbm],
-        out_specs=(vmem, vmem, vmem),
+        out_shape=[pltpu.VMEM(*shape) for shape in shapes],
+        in_specs=[hbm] * 10,
+        out_specs=[vmem] * 3,
         scratch_shapes=scratch,
         compiler_params=pltpu.CompilerParams(
-            collective_id=0, has_side_effects=True, vmem_limit_bytes=60 * 1024 * 1024
+            collective_id=0, has_side_effects=True, vmem_limit_bytes=room
         ),
     )(features, occupancy, coords, norm_gains, bias_tables, w_qkv, w_out, w_up, w_down, grad_out)
+    return tuple(pl.pallas_call(
+        finish,
+        out_shape=[jax.ShapeDtypeStruct(*shape) for shape in shapes],
+        in_specs=[vmem] * 3,
+        out_specs=[vmem] * 3,
+        compiler_params=pltpu.CompilerParams(vmem_limit_bytes=2 * 1024 * 1024),
+    )(*results))
 
 
 def solution(mesh):

time: 37.1 us -> 27.8 us (0.75)
  Pallas kernels: 32.1 us -> 27.1 us
  local copies, waits for them, and re-layouts: 4.11 us -> 0 us
    pallas_call x1 -> x2, Pallas kernels: 32.1 us -> 27.1 us  [the longest x1 26.4 us: on_device(): pl.pallas_call(partial(kernel, nx, ny), out_shape=[pltpu.VMEM(*shape) for...]
    unnamed x8 -> x0, local copies, waits for them, and re-layouts: 4.11 us -> none
where the time goes in v2:
time: 27.8 us; the launch traced here: 27.7 us
  Pallas kernels  27.1 us (97%)
  between operations  0.64 us (2%)
    pallas_call x1, Pallas kernels, on_device(): pl.pallas_call(partial(kernel, nx, ny), out_shape=[pltpu.VMEM(*shape) for...  26.4 us
    pallas_call x1, Pallas kernels, on_device(): pl.pallas_call(finish, out_shape=[jax.ShapeDtypeStruct(*shape) for shape...  0.66 us

profile of v2, /device:TPU:0, one launch (start us, length us, event | category | flops | bytes accessed | tf_op | source)
XLA Modules:
  0.0 27.7 jit_solution(12605854109456813375)
XLA Ops:
  0.6 26.4 %shard_map.121 = (bf16[1,1,128,256]{3,2,1,0:T(8,128)(2,1)S(1)}, bf16[1,1,128,256]{3,2,1,0:T(8,128)(2,1)S(1)}, f32[2,3,8,15]{3,2,1,0:T(8,128)S(1)}) custom-call(bf16[1,1,128,256]{3,2,1,0:T(8,128)(2,1)} %feat.1, s32[1,1,128]{2,1,0:T(1,128)} %occ_h.1, s32[1,3,1,128]{3,2,1,0:T(1,128)} %bitcast.1, f32[2,2,256]{2,1,0:T(2,128)} %gains_h.1, ...), custom_call_target="tpu_custom_call" | custom-call | tf_op jit(solution)/shard_map/pallas_call | solution.py:496
  27.0 0.7 %shard_map.122 = (bf16[1,1,128,256]{3,2,1,0:T(8,128)(2,1)}, bf16[1,1,128,256]{3,2,1,0:T(8,128)(2,1)}, f32[2,3,8,15]{3,2,1,0:T(8,128)}) custom-call(bf16[1,1,128,256]{3,2,1,0:T(8,128)(2,1)S(1)} %get-tuple-element.6.points_in, bf16[1,1,128,256]{3,2,1,0:T(8,128)(2,1)S(1)} %get-tuple-element.7.grads_in, f32[2,3,8,15]{3,2,1,0:T(8,128)S(1)} %get-tuple-element.8.tables_in), custom_call_target="tpu_custom_call" | custom-call | tf_op jit(solution)/shard_map/pallas_call | solution.py:506

commit v3 on v2

--- a/solution.py
+++ b/solution.py
@@ -52,8 +52,8 @@
     x_v, g_v, wqkv_v, wout_v, wup_v, wdown_v,
     meta, meta_recv, g_roll, first, rolled, second, back, grad_mid, grad_first,
     table_pad, band, left_bias, diag, probs, proj, keys_t, unit_one, unit_two,
-    rstd_one, rstd_two, gelu_in, expanded_v, cot_wide_v, onehot_s, onehot_t, score_cot, cot_pair,
-    q_stack, mix_stack,
+    rstd_one, rstd_two, gelu_in, expanded_v, cot_wide_v, onehot_s, onehot_t, cot_pair,
+    q_stack, v_stack, mix_stack,
     t_send, t_recv_x, t_mid, t_recv_y,
     load_sem, send_sem, recv_sem, tx_send, tx_recv, ty_send, ty_recv,
 ):
@@ -244,6 +244,10 @@
                 GELU_SCALE + (3.0 * GELU_SCALE * GELU_CUBE) * square
             )
 
+    def stack_parts(k):
+        q_stack[k] = stacked(proj[k, :, 0:width])
+        v_stack[k] = stacked(proj[k, :, 2 * width:])
+
     def pull_wide(k, cotangent):
         for cut in chunks:
             cot_wide_v[k, :, cut] = dot_nt(cotangent, wdown_v[k, cut, :]).astype(BF16)
@@ -259,7 +263,7 @@
         )
         cot_mixed = dot_nt(cot_middle.astype(BF16), wout_v[k]).astype(BF16)
         mix_stack[...] = stacked(cot_mixed)
-        cot_all = dot_nt(stacked(proj[k, :, 2 * width:]), cot_mixed)
+        cot_all = dot_nt(v_stack[k], cot_mixed)
         for h in range(heads):
             here = slice(h * slots, (h + 1) * slots)
             cot_probs = cot_all[here].astype(BF16).astype(F32)
@@ -267,27 +271,18 @@
             product = weights * cot_probs
             total = jnp.sum(product, axis=0, keepdims=True)
             high, low = split_two(product - weights * total)
-            cot_pair[here, 0:slots] = high
-            cot_pair[here, slots:2 * slots] = low
+            cot_pair[0:slots, here] = high
+            cot_pair[slots:2 * slots, here] = low
         return cot_middle
 
     def table_sums(k):
         hot_twice = jnp.concatenate([onehot_s[k], onehot_s[k]], axis=0)
         hot_t_twice = jnp.concatenate([onehot_t[k], onehot_t[k]], axis=1)
-        by_key = dot_nn(cot_pair[...], hot_twice)
-        key_high, key_low = split_two(by_key)
-        pair = jnp.concatenate(
-            [
-                jnp.concatenate(
-                    [part[h * slots:(h + 1) * slots] for h in range(heads)], axis=1
-                )
-                for part in (key_high, key_low)
-            ],
-            axis=0,
+        by_cell = dot_nn(hot_t_twice, cot_pair[...])
+        by_cell = jnp.concatenate(
+            [by_cell[:, h * slots:(h + 1) * slots] for h in range(heads)], axis=0
         )
-        pairs_sum = dot_nn(hot_t_twice, pair)
-        for h in range(heads):
-            diag[h * pad_rows:(h + 1) * pad_rows, :] = pairs_sum[:, h * slots:(h + 1) * slots]
+        diag[...] = dot_nn(jnp.concatenate(split_two(by_cell), axis=1), hot_twice)
         sums = []
         for e in range(3):
             inside = (lane >= e * cells) & (lane < (e + 1) * cells)
@@ -304,12 +299,10 @@
     def pull_proj(k):
         pieces = []
         for h in range(heads):
-            high = cot_pair[h * slots:(h + 1) * slots, 0:slots]
-            score_cot[:, h * slots:(h + 1) * slots] = high
+            high = cot_pair[0:slots, h * slots:(h + 1) * slots]
             pieces.append(dot_nn(keys_t[k, h * head_size:(h + 1) * head_size], high))
-        q_stack[...] = stacked(proj[k, :, 0:width])
         cot_queries = (jnp.transpose(jnp.concatenate(pieces, axis=0)) * scale).astype(BF16)
-        cot_keys = (dot_nn(score_cot[...], q_stack[...]) * scale).astype(BF16)
+        cot_keys = (dot_nn(cot_pair[0:slots, :], q_stack[k]) * scale).astype(BF16)
         probs_wide = jnp.concatenate(
             [probs[k, h * slots:(h + 1) * slots] for h in range(heads)], axis=1
         )
@@ -328,10 +321,10 @@
     meta[0:1, :] = occ[0]
     for e in range(3):
         meta[e + 1:e + 2, :] = coords[0, e]
+    occupied = prepare_bias(0, occ[0], [coords[0, e] for e in range(3)])
     loads[0].wait()
     hidden = x_v[...].astype(F32)
     values_t = attention_head(0, hidden)
-    occupied = prepare_bias(0, occ[0], [coords[0, e] for e in range(3)])
     middle = attention_part(0, hidden, values_t)
 
     pl.semaphore_wait(barrier, nx + ny)
@@ -378,12 +371,14 @@
     hidden = rolled[...].astype(F32)
     middle = attention_part(1, hidden, attention_head(1, hidden))
     feed_part(1, middle, True)
+    stack_parts(1)
     cot_middle = pull_scores(1, grad_in)
     grad_mid[...] = pull_input(1, pull_proj(1), cot_middle)
     mid_copies = roll_backward(grad_mid, grad_first, 12)
     second[...] = (middle + dot_nn(expanded_v[1], wdown_v[1])).astype(BF16)
     second_copies = roll_backward(second, back, 9)
     table_sums(1)
+    stack_parts(0)
     for copy in mid_copies:
         copy.wait()
 
@@ -405,24 +400,23 @@
     pull_wide(0, cotangent)
     cot_middle = pull_scores(0, cotangent)
     table_sums(0)
-    table_copies = exchange(t_send, t_recv_x, tx_send, tx_recv, i, nx, lambda other: (other, j))
+    table_copies = exchange(t_send, t_recv_y, ty_send, ty_recv, j, ny, lambda other: (i, other))
     cot_proj = pull_proj(0)
+    grad_points[0, 0] = pull_input(0, cot_proj, cot_middle)
+    for copy in second_copies:
+        copy.wait()
+    out_points[0, 0] = (back[...].astype(F32) * occupied).astype(BF16)
     for copy in table_copies:
+        copy.wait()
+    total = t_recv_y[0]
+    for n in range(1, ny):
+        total = total + t_recv_y[n]
+    t_mid[...] = total
+    for copy in exchange(t_mid, t_recv_x, tx_send, tx_recv, i, nx, lambda other: (other, j)):
         copy.wait()
     total = t_recv_x[0]
     for n in range(1, nx):
         total = total + t_recv_x[n]
-    t_mid[...] = total
-    table_copies = exchange(t_mid, t_recv_y, ty_send, ty_recv, j, ny, lambda other: (i, other))
-    grad_points[0, 0] = pull_input(0, cot_proj, cot_middle)
-    for copy in second_copies:
-        copy.wait()
-    out_points[0, 0] = (back[...].astype(F32) * occupied).astype(BF16)
-    for copy in table_copies:
-        copy.wait()
-    total = t_recv_y[0]
-    for n in range(1, ny):
-        total = total + t_recv_y[n]
     for k in range(2):
         for e in range(3):
             tile = total[k * heads:(k + 1) * heads]
@@ -480,9 +474,9 @@
         pltpu.VMEM((2, slots, hidden), BF16),
         pltpu.VMEM((2, slots, slots), BF16),
         pltpu.VMEM((2, 32, slots), BF16),
-        pltpu.VMEM((slots, heads * slots), BF16),
-        pltpu.VMEM((heads * slots, 2 * slots), BF16),
-        pltpu.VMEM((heads * slots, width), BF16),
+        pltpu.VMEM((2 * slots, heads * slots), BF16),
+        pltpu.VMEM((2, heads * slots, width), BF16),
+        pltpu.VMEM((2, heads * slots, width), BF16),
         pltpu.VMEM((heads * slots, width), BF16),
         pltpu.VMEM((2 * heads, slots), F32),
         pltpu.VMEM((nx, 2 * heads, slots), F32),

time: 27.8 us -> 27.9 us (level)
  no operation moved by 1% of the time
where the time goes in v3:
time: 27.9 us; the launch traced here: 27.8 us
  Pallas kernels  27.1 us (97%)
  between operations  0.64 us (2%)
    pallas_call x1, Pallas kernels, on_device(): pl.pallas_call(partial(kernel, nx, ny), out_shape=[pltpu.VMEM(*shape) for...  26.5 us
    pallas_call x1, Pallas kernels, on_device(): pl.pallas_call(finish, out_shape=[jax.ShapeDtypeStruct(*shape) for shape...  0.66 us

profile of v3, /device:TPU:0, one launch (start us, length us, event | category | flops | bytes accessed | tf_op | source)
XLA Modules:
  0.0 27.8 jit_solution(9649301305984394776)
XLA Ops:
  0.6 26.5 %shard_map.121 = (bf16[1,1,128,256]{3,2,1,0:T(8,128)(2,1)S(1)}, bf16[1,1,128,256]{3,2,1,0:T(8,128)(2,1)S(1)}, f32[2,3,8,15]{3,2,1,0:T(8,128)S(1)}) custom-call(bf16[1,1,128,256]{3,2,1,0:T(8,128)(2,1)} %feat.1, s32[1,1,128]{2,1,0:T(1,128)} %occ_h.1, s32[1,3,1,128]{3,2,1,0:T(1,128)} %bitcast.1, f32[2,2,256]{2,1,0:T(2,128)} %gains_h.1, ...), custom_call_target="tpu_custom_call" | custom-call | tf_op jit(solution)/shard_map/pallas_call | solution.py:490
  27.1 0.7 %shard_map.122 = (bf16[1,1,128,256]{3,2,1,0:T(8,128)(2,1)}, bf16[1,1,128,256]{3,2,1,0:T(8,128)(2,1)}, f32[2,3,8,15]{3,2,1,0:T(8,128)}) custom-call(bf16[1,1,128,256]{3,2,1,0:T(8,128)(2,1)S(1)} %get-tuple-element.6.points_in, bf16[1,1,128,256]{3,2,1,0:T(8,128)(2,1)S(1)} %get-tuple-element.7.grads_in, f32[2,3,8,15]{3,2,1,0:T(8,128)S(1)} %get-tuple-element.8.tables_in), custom_call_target="tpu_custom_call" | custom-call | tf_op jit(solution)/shard_map/pallas_call | solution.py:500

commit v4 on v3

--- a/solution.py
+++ b/solution.py
@@ -248,15 +248,20 @@
         q_stack[k] = stacked(proj[k, :, 0:width])
         v_stack[k] = stacked(proj[k, :, 2 * width:])
 
-    def pull_wide(k, cotangent):
+    def pull_wide(k, cotangent, with_slope):
         for cut in chunks:
-            cot_wide_v[k, :, cut] = dot_nt(cotangent, wdown_v[k, cut, :]).astype(BF16)
-
-    def pull_scores(k, cotangent):
+            cot_wide = dot_nt(cotangent, wdown_v[k, cut, :]).astype(BF16)
+            if with_slope:
+                cot_wide = (cot_wide.astype(F32) * gelu_in[k, :, cut]).astype(BF16)
+            cot_wide_v[k, :, cut] = cot_wide
+
+    def scale_wide(k):
         for cut in chunks:
             cot_wide_v[k, :, cut] = (
                 cot_wide_v[k, :, cut].astype(F32) * gelu_in[k, :, cut]
             ).astype(BF16)
+
+    def pull_scores(k, cotangent):
         cot_normed = dot_nt(cot_wide_v[k], wup_v[k]).astype(BF16).astype(F32)
         cot_middle = cotangent.astype(F32) + norm_pullback(
             cot_normed, gains[k, 1:2], unit_two[k], rstd_two[k]
@@ -321,10 +326,10 @@
     meta[0:1, :] = occ[0]
     for e in range(3):
         meta[e + 1:e + 2, :] = coords[0, e]
-    occupied = prepare_bias(0, occ[0], [coords[0, e] for e in range(3)])
     loads[0].wait()
     hidden = x_v[...].astype(F32)
     values_t = attention_head(0, hidden)
+    occupied = prepare_bias(0, occ[0], [coords[0, e] for e in range(3)])
     middle = attention_part(0, hidden, values_t)
 
     pl.semaphore_wait(barrier, nx + ny)
@@ -365,13 +370,14 @@
         copy.wait()
     grad_in = (g_roll[...].astype(F32) * shifted_occupied).astype(BF16)
     loads[8].wait()
-    pull_wide(1, grad_in)
+    pull_wide(1, grad_in, False)
     for copy in first_copies:
         copy.wait()
     hidden = rolled[...].astype(F32)
     middle = attention_part(1, hidden, attention_head(1, hidden))
     feed_part(1, middle, True)
     stack_parts(1)
+    scale_wide(1)
     cot_middle = pull_scores(1, grad_in)
     grad_mid[...] = pull_input(1, pull_proj(1), cot_middle)
     mid_copies = roll_backward(grad_mid, grad_first, 12)
@@ -397,11 +403,18 @@
         return copies
 
     cotangent = grad_first[...]
-    pull_wide(0, cotangent)
+    pull_wide(0, cotangent, True)
     cot_middle = pull_scores(0, cotangent)
     table_sums(0)
-    table_copies = exchange(t_send, t_recv_y, ty_send, ty_recv, j, ny, lambda other: (i, other))
+    table_copies = exchange(t_send, t_recv_x, tx_send, tx_recv, i, nx, lambda other: (other, j))
     cot_proj = pull_proj(0)
+    for copy in table_copies:
+        copy.wait()
+    total = t_recv_x[0]
+    for n in range(1, nx):
+        total = total + t_recv_x[n]
+    t_mid[...] = total
+    table_copies = exchange(t_mid, t_recv_y, ty_send, ty_recv, j, ny, lambda other: (i, other))
     grad_points[0, 0] = pull_input(0, cot_proj, cot_middle)
     for copy in second_copies:
         copy.wait()
@@ -411,12 +424,6 @@
     total = t_recv_y[0]
     for n in range(1, ny):
         total = total + t_recv_y[n]
-    t_mid[...] = total
-    for copy in exchange(t_mid, t_recv_x, tx_send, tx_recv, i, nx, lambda other: (other, j)):
-        copy.wait()
-    total = t_recv_x[0]
-    for n in range(1, nx):
-        total = total + t_recv_x[n]
     for k in range(2):
         for e in range(3):
             tile = total[k * heads:(k + 1) * heads]

time: 27.9 us -> 27.9 us (level)
  no operation moved by 1% of the time
where the time goes in v4:
time: 27.9 us; the launch traced here: 27.7 us
  Pallas kernels  27.1 us (97%)
  between operations  0.64 us (2%)
    pallas_call x1, Pallas kernels, on_device(): pl.pallas_call(partial(kernel, nx, ny), out_shape=[pltpu.VMEM(*shape) for...  26.4 us
    pallas_call x1, Pallas kernels, on_device(): pl.pallas_call(finish, out_shape=[jax.ShapeDtypeStruct(*shape) for shape...  0.66 us

profile of v4, /device:TPU:0, one launch (start us, length us, event | category | flops | bytes accessed | tf_op | source)
XLA Modules:
  0.0 27.7 jit_solution(1530548789117197601)
XLA Ops:
  0.6 26.4 %shard_map.121 = (bf16[1,1,128,256]{3,2,1,0:T(8,128)(2,1)S(1)}, bf16[1,1,128,256]{3,2,1,0:T(8,128)(2,1)S(1)}, f32[2,3,8,15]{3,2,1,0:T(8,128)S(1)}) custom-call(bf16[1,1,128,256]{3,2,1,0:T(8,128)(2,1)} %feat.1, s32[1,1,128]{2,1,0:T(1,128)} %occ_h.1, s32[1,3,1,128]{3,2,1,0:T(1,128)} %bitcast.1, f32[2,2,256]{2,1,0:T(2,128)} %gains_h.1, ...), custom_call_target="tpu_custom_call" | custom-call | tf_op jit(solution)/shard_map/pallas_call | solution.py:497
  27.0 0.7 %shard_map.122 = (bf16[1,1,128,256]{3,2,1,0:T(8,128)(2,1)}, bf16[1,1,128,256]{3,2,1,0:T(8,128)(2,1)}, f32[2,3,8,15]{3,2,1,0:T(8,128)}) custom-call(bf16[1,1,128,256]{3,2,1,0:T(8,128)(2,1)S(1)} %get-tuple-element.6.points_in, bf16[1,1,128,256]{3,2,1,0:T(8,128)(2,1)S(1)} %get-tuple-element.7.grads_in, f32[2,3,8,15]{3,2,1,0:T(8,128)S(1)} %get-tuple-element.8.tables_in), custom_call_target="tpu_custom_call" | custom-call | tf_op jit(solution)/shard_map/pallas_call | solution.py:507
